TPU v7x, 256 devices: a whole 4x4x8 slice. The times are simulated.
256 devices in a mesh: tile: 32 (over x, z_hi, y), mode: 8 (over z_lo, core).
Axes of the slice: x: 4, y: 4, z: 8 (z_hi: 2, z_lo: 4; z = z_hi * 4 + z_lo), core: 2. Of those that a mesh axis runs over, the one named last changes fastest.
Arguments:
- object_field: float32 [2, 8192, 512], P(None, 'tile'), may hold values from -4.2 to 4.2
- probe: float32 [8, 2, 256, 256], P('mode'), may hold values from -2.1 to 2.1
- positions: int32 [2, 64, 2], P(None, 'tile'), may hold values from 0 to 7936, as said below
- measured: float32 [2, 64, 256, 256], P(None, 'tile'), may hold values from 0.1 to 30
Outputs:
- refined_object: float32 [2, 8192, 512], P(None, 'tile')
- refined_probe: float32 [8, 2, 256, 256], P('mode')
Inputs may be any that keep to these rules, and one draw needn't show every extreme that they name: positions[b, j] = (row, column). Position j belongs to tile t = j // 2; its row lies from t * 256 - 256 / 2 to t * 256 - 256 / 2 + 256, both ends reached in some tile, and every pattern lies inside the object of 8192 x 512.
All inputs are finite; a program needn't handle non-finite values.
Results may differ from a plain program's by a relative error of at most 0.0001.
Values sent between devices are 32-bit elements; how exact they have to be, the bound alone decides.
A program may use at most 64 MiB of HBM per device.

v0:
```python
import math

import jax
import jax.numpy as jnp
from jax import lax
from jax.sharding import PartitionSpec as P


def padded(block, sides, width):
    for axis, dim in sides:
        count = lax.axis_size(axis)
        forward = [(i, i + 1) for i in range(count - 1)]
        backward = [(target, source) for source, target in forward]
        low = lax.ppermute(
            lax.slice_in_dim(block, block.shape[dim] - width, None, axis=dim), axis, forward
        )
        high = lax.ppermute(lax.slice_in_dim(block, 0, width, axis=dim), axis, backward)
        block = jnp.concatenate([low, block, high], axis=dim)
    return block


def tables(length):
    index_values = jnp.arange(length, dtype=jnp.int32)
    product = index_values[:, None] * index_values[None, :] % length
    angles = product.astype(jnp.float32) * (2.0 * math.pi / length)
    scaling = 1.0 / math.sqrt(length)
    return (jnp.cos(angles) * scaling, jnp.sin(angles) * scaling)


def apply_left(matrix, target):
    return jnp.einsum("ab,pbc->pac", matrix, target, precision=lax.Precision.HIGHEST)


def apply_right(target, matrix):
    return jnp.einsum("pab,bc->pac", target, matrix, precision=lax.Precision.HIGHEST)


def transform(real_part, imag_part, cosine, sine_table, direction):
    left_real = apply_left(cosine, real_part) + direction * apply_left(sine_table, imag_part)
    left_imag = apply_left(cosine, imag_part) - direction * apply_left(sine_table, real_part)
    out_real = apply_right(left_real, cosine) + direction * apply_right(left_imag, sine_table)
    out_imag = apply_right(left_imag, cosine) - direction * apply_right(left_real, sine_table)
    return (out_real, out_imag)


def place_add(target, placed, row_start, col_start):
    zero_index = jnp.int32(0)
    current = lax.dynamic_slice(target, (zero_index, row_start, col_start), placed.shape)
    return lax.dynamic_update_slice(target, current + placed, (zero_index, row_start, col_start))


def shards(object_field, probe, positions, measured):
    strip_rows = object_field.shape[1]
    object_width = object_field.shape[2]
    pattern = probe.shape[2]
    half_pattern = pattern // 2
    count = positions.shape[1]
    cosine, sine_table = tables(pattern)
    tile_index = lax.axis_index("tile")
    offset = tile_index * strip_rows - half_pattern
    for minibatch in range(measured.shape[0]):
        extended = padded(object_field, (("tile", 1),), half_pattern)
        row_offsets = positions[minibatch, :, 0] - offset
        column_offsets = positions[minibatch, :, 1]

        def cut_one(row_start, col_start):
            return lax.dynamic_slice(
                extended, (jnp.int32(0), row_start, col_start), (2, pattern, pattern)
            )

        patches = jax.vmap(cut_one)(row_offsets, column_offsets)
        obj_real = patches[:, 0]
        obj_imag = patches[:, 1]
        mode_index = 0
        probe_real = probe[mode_index, 0]
        probe_imag = probe[mode_index, 1]
        exit_real = probe_real * obj_real - probe_imag * obj_imag
        exit_imag = probe_real * obj_imag + probe_imag * obj_real
        far_real, far_imag = transform(exit_real, exit_imag, cosine, sine_table, 1.0)
        far_fields = [(far_real, far_imag)]
        local_power = far_real * far_real + far_imag * far_imag
        observed = measured[minibatch]
        intensity = lax.psum(local_power, "mode")
        modulus = jnp.sqrt((observed + 1.0) / (intensity + 1.0)) - 1.0
        mode_index = 0
        probe_real = probe[mode_index, 0]
        probe_imag = probe[mode_index, 1]
        far_real, far_imag = far_fields[mode_index]
        chi_real, chi_imag = transform(
            modulus * far_real, modulus * far_imag, cosine, sine_table, -1.0
        )
        grad_real = probe_real * chi_real + probe_imag * chi_imag
        grad_imag = probe_real * chi_imag - probe_imag * chi_real
        probe_power = probe_real * probe_real + probe_imag * probe_imag
        step_real = jnp.sum(obj_real * chi_real + obj_imag * chi_imag, axis=0)
        step_imag = jnp.sum(obj_real * chi_imag - obj_imag * chi_real, axis=0)
        probe_steps = [jnp.stack([step_real, step_imag])]
        coverage = jnp.sum(obj_real * obj_real + obj_imag * obj_imag, axis=0)
        accumulated = jnp.zeros((3, strip_rows + pattern, object_width), jnp.float32)
        for position in range(count):
            placed = jnp.stack([grad_real[position], grad_imag[position], probe_power])
            accumulated = place_add(
                accumulated, placed, row_offsets[position], column_offsets[position]
            )
        rim_rows = jnp.concatenate(
            [accumulated[:, :half_pattern], accumulated[:, strip_rows + half_pattern :]], axis=1
        )
        received = padded(rim_rows, (("tile", 1),), half_pattern)
        own_strip = accumulated[:, half_pattern : half_pattern + strip_rows]
        own_strip = own_strip.at[:, :half_pattern].add(received[:, :half_pattern])
        own_strip = own_strip.at[:, strip_rows - half_pattern :].add(
            received[:, pattern + half_pattern :]
        )
        summed = lax.psum(own_strip, "mode")
        divisor = summed[2] + 1.0
        object_field = jnp.stack(
            [object_field[0] + summed[0] / divisor, object_field[1] + summed[1] / divisor]
        )
        step_stack = jnp.stack(probe_steps)
        step_total, coverage_total = lax.psum((step_stack, coverage), "tile")
        probe = probe + step_total / (coverage_total + 1.0)
    return (object_field, probe)


def solution(mesh):
    in_specs = (
        P(None, "tile", None),
        P("mode", None, None, None),
        P(None, "tile", None),
        P(None, "tile", None, None),
    )
    out_specs = (P(None, "tile", None), P("mode", None, None, None))
    return jax.shard_map(shards, mesh=mesh, in_specs=in_specs, out_specs=out_specs, check_vma=False)
```

profile of v0, /device:TPU:1, one launch (start us, length us, event | category | flops | bytes accessed | tf_op | source)
XLA Modules:
  0.0 1431.6 jit_solution(11666397501852633452)
XLA Ops:
  8.6 4.1 collective-permute-start
  15.2 8.0 collective-permute-done
  24.0 3.1 collective-permute-done.1
  28.6 4.5 while.6
  33.1 2.9 fusion.92
  36.0 2.8 fusion.96
  38.9 1.9 fusion.14
  40.8 1.9 fusion.15
  46.3 2.3 convolution_add_fusion.2
  48.6 2.6 multiply_add_fusion.3
  60.0 81.7 %all-reduce.9.cloned.1.call-done = f32[2,256,256]{2,1,0:T(8,128)} async-done(((f32[2,256,256]{2,1,0:T(8,128)}), f32[2,256,256]{2,1,0:T(8,128)}) %all-reduce.9.cloned.1.call-update) | async-done | bytes 524304 | tf_op jit(solution)/shard_map/psum | solution.py:83
  146.8 1.9 fusion.11
  150.5 1.9 fusion.13
  154.2 2.0 fusion.9
  156.2 3.0 fusion.40
  162.0 10.6 dynamic_update_slice.12
  172.7 2.2 fusion.17
  174.9 10.3 dynamic_update_slice.13
  185.4 8.5 collective-permute-start.2
  196.4 11.1 collective-permute-done.2
  208.5 2.8 collective-permute-done.3
  211.4 2.2 fusion.20
  214.6 98.3 %all-reduce.11.cloned.1.call-done = f32[3,256,512]{2,1,0:T(8,128)} async-done(((f32[3,256,512]{2,1,0:T(8,128)}), f32[3,256,512]{2,1,0:T(8,128)}) %all-reduce.11.cloned.1.call-update) | async-done | bytes 1572880 | tf_op jit(solution)/shard_map/psum | solution.py:114
  314.7 4.1 collective-permute-start.4
  320.1 410.0 %all-reduce.19.cloned.1.call-done = (f32[1,2,256,256]{3,2,1,0:T(8,128)}, f32[256,256]{1,0:T(8,128)}) async-done(((f32[1,2,256,256]{3,2,1,0:T(8,128)}, f32[256,256]{1,0:T(8,128)}), (f32[1,2,256,256]{3,2,1,0:T(8,128)}, f32[256,256]{1,0:T(8,128)})) %all-reduce.19.cloned.1.call-update) | async-done | bytes 786448 | tf_op jit(solution)/shard_map/psum | solution.py:120
  734.7 4.7 while.7
  739.4 2.9 fusion.76
  742.3 2.8 fusion.80
  745.1 1.9 fusion.6
  747.0 1.9 fusion.7
  752.6 2.2 convolution_add_fusion
  754.8 2.6 multiply_add_fusion.1
  764.8 83.7 %all-reduce.13.cloned.1.call-done = f32[2,256,256]{2,1,0:T(8,128)} async-done(((f32[2,256,256]{2,1,0:T(8,128)}), f32[2,256,256]{2,1,0:T(8,128)}) %all-reduce.13.cloned.1.call-update) | async-done | bytes 524304 | tf_op jit(solution)/shard_map/psum | solution.py:83
  853.6 1.9 fusion.3
  855.4 1.9 fusion.5
  861.0 2.0 fusion.1
  863.0 3.0 fusion.30
  868.8 11.1 dynamic_update_slice.14
  879.9 2.2 fusion.16
  882.1 10.4 dynamic_update_slice.15
  893.8 2.9 collective-permute-start.6
  900.2 9.6 collective-permute-done.6
  909.8 2.2 fusion.19
  912.0 7.0 collective-permute-done.7
  918.9 2.4 fusion.18
  921.4 401.4 %all-reduce.17.cloned.1.call-done = (f32[1,2,256,256]{3,2,1,0:T(8,128)}, f32[256,256]{1,0:T(8,128)}) async-done(((f32[1,2,256,256]{3,2,1,0:T(8,128)}, f32[256,256]{1,0:T(8,128)}), (f32[1,2,256,256]{3,2,1,0:T(8,128)}, f32[256,256]{1,0:T(8,128)})) %all-reduce.17.cloned.1.call-update) | async-done | bytes 786448 | tf_op jit(solution)/shard_map/psum | solution.py:120
  1323.7 1.9 divide_add_fusion
  1325.6 96.3 %all-reduce.15.cloned.1.call-done = f32[3,256,512]{2,1,0:T(8,128)} async-done(((f32[3,256,512]{2,1,0:T(8,128)}), f32[3,256,512]{2,1,0:T(8,128)}) %all-reduce.15.cloned.1.call-update) | async-done | bytes 1572880 | tf_op jit(solution)/shard_map/psum | solution.py:114
  (122 shorter events, 67.6 us)
Async XLA Ops:
  7.2 20.0 %copy-start = (f32[2,256,512]{2,1,0:T(8,128)S(1)}, f32[2,256,512]{2,1,0:T(8,128)}, u32[]{:S(2)}) copy-start(f32[2,256,512]{2,1,0:T(8,128)} %param.12) | copy-start | bytes 3145732
  7.2 6.8 copy-start.19
  7.2 7.2 copy-start.12
  7.2 134.5 %all-reduce.9.cloned.1.call-start = ((), (), s32[]{:S(2)}) async-start(), calls=%async_computation | async-start | bytes 1048576 | tf_op jit(solution)/shard_map/psum | solution.py:83
  8.6 14.6 %collective-permute-start = (f32[2,128,512]{2,1,0:T(8,128)S(1)}, f32[2,128,512]{2,1,0:T(8,128)S(1)}, u32[]{:S(2)}, u32[]{:S(2)}) collective-permute-start(f32[2,128,512]{2,1,0:T(8,128)S(1)} %get-tuple-element.128), channel_id=1, source_target_pairs={{0,8},{8,16},{16,24},{24,32},{32,40},{40,48},{48,56},{56,64},{64,7... | collective-permute-start | bytes 1572872 | tf_op jit(solution)/shard_map/ppermute | solution.py:14
  12.7 14.5 %collective-permute-start.1 = (f32[2,128,512]{2,1,0:T(8,128)S(1)}, f32[2,128,512]{2,1,0:T(8,128)}, u32[]{:S(2)}, u32[]{:S(2)}) collective-permute-start(f32[2,128,512]{2,1,0:T(8,128)S(1)} %get-tuple-element.129), channel_id=1, source_target_pairs={{8,0},{16,8},{24,16},{32,24},{40,32},{48,40},{56,48},{64,56},{72,6... | collective-permute-start | bytes 1572872 | tf_op jit(solution)/shard_map/ppermute | solution.py:17
  23.2 0.8 copy-start.18
  33.1 5.7 copy-start.8
  51.3 261.7 %all-reduce.11.cloned.1.call-start = ((), (), s32[]{:S(2)}) async-start(), calls=%async_computation.1 | async-start | bytes 3145728 | tf_op jit(solution)/shard_map/psum | solution.py:114
  159.2 1.5 copy-start.10
  185.4 22.1 %collective-permute-start.2 = (f32[3,128,512]{2,1,0:T(8,128)S(1)}, f32[3,128,512]{2,1,0:T(8,128)S(1)}, u32[]{:S(2)}, u32[]{:S(2)}) collective-permute-start(f32[3,128,512]{2,1,0:T(8,128)S(1)} %get-tuple-element.113), channel_id=1, source_target_pairs={{0,8},{8,16},{16,24},{24,32},{32,40},{40,48},{48,56},{56,64},{64,7... | collective-permute-start | bytes 2359304 | tf_op jit(solution)/shard_map/ppermute | solution.py:14
  193.8 17.5 %collective-permute-start.3 = (f32[3,128,512]{2,1,0:T(8,128)S(1)}, f32[3,128,512]{2,1,0:T(8,128)S(1)}, u32[]{:S(2)}, u32[]{:S(2)}) collective-permute-start(f32[3,128,512]{2,1,0:T(8,128)S(1)} %get-tuple-element.112), channel_id=1, source_target_pairs={{8,0},{16,8},{24,16},{32,24},{40,32},{48,40},{56,48},{64,56},{72,6... | collective-permute-start | bytes 2359304 | tf_op jit(solution)/shard_map/ppermute | solution.py:17
  208.5 5.1 copy-start.14
  208.5 5.1 copy-start.15
  213.5 99.4 %copy-start.1 = (f32[2,256,512]{2,1,0:T(8,128)S(1)}, f32[2,256,512]{2,1,0:T(8,128)}, u32[]{:S(2)}) copy-start(f32[2,256,512]{2,1,0:T(8,128)} %param.12) | copy-start | bytes 3145732
  213.6 516.5 %all-reduce.19.cloned.1.call-start = ((), (), s32[]{:S(2)}) async-start(), calls=%async_computation.5 | async-start | bytes 1572864 | tf_op jit(solution)/shard_map/psum | solution.py:120
  214.5 634.0 %all-reduce.13.cloned.1.call-start = ((), (), s32[]{:S(2)}) async-start(), calls=%async_computation.2 | async-start | bytes 1048576 | tf_op jit(solution)/shard_map/psum | solution.py:83
  314.6 418.6 %copy-start.2 = (f32[1,256,512]{2,1,0:T(8,128)}, f32[1,256,512]{2,1,0:T(8,128)S(1)}, u32[]{:S(2)}) copy-start(f32[1,256,512]{2,1,0:T(8,128)S(1)} %get-tuple-element.114) | copy-start | bytes 1572868
  314.6 418.6 %copy-start.4 = (f32[1,256,512]{2,1,0:T(8,128)}, f32[1,256,512]{2,1,0:T(8,128)S(1)}, u32[]{:S(2)}) copy-start(f32[1,256,512]{2,1,0:T(8,128)S(1)} %get-tuple-element.115) | copy-start | bytes 1572868
  314.6 416.4 %copy-start.13 = (f32[1,2,256,256]{3,2,1,0:T(8,128)S(1)}, f32[1,2,256,256]{3,2,1,0:T(8,128)}, u32[]{:S(2)}) copy-start(f32[1,2,256,256]{3,2,1,0:T(8,128)} %param.13) | copy-start | bytes 1572868
  314.7 418.5 %collective-permute-start.4 = (f32[2,128,512]{2,1,0:T(8,128)S(1)}, f32[2,128,512]{2,1,0:T(8,128)}, u32[]{:S(2)}, u32[]{:S(2)}) collective-permute-start(f32[2,128,512]{2,1,0:T(8,128)S(1)} %get-tuple-element.124), channel_id=1, source_target_pairs={{0,8},{8,16},{16,24},{24,32},{32,40},{40,48},{48,56},{56,64},{64,7... | collective-permute-start | bytes 1572872 | tf_op jit(solution)/shard_map/ppermute | solution.py:14
  318.8 414.5 %collective-permute-start.5 = (f32[2,128,512]{2,1,0:T(8,128)S(1)}, f32[2,128,512]{2,1,0:T(8,128)}, u32[]{:S(2)}, u32[]{:S(2)}) collective-permute-start(f32[2,128,512]{2,1,0:T(8,128)S(1)} %get-tuple-element.125), channel_id=1, source_target_pairs={{8,0},{16,8},{24,16},{32,24},{40,32},{48,40},{56,48},{64,56},{72,6... | collective-permute-start | bytes 1572872 | tf_op jit(solution)/shard_map/ppermute | solution.py:17
  732.2 1.0 copy-start.6
  739.4 5.7 copy-start.9
  757.5 565.3 %all-reduce.17.cloned.1.call-start = ((), (), s32[]{:S(2)}) async-start(), calls=%async_computation.4 | async-start | bytes 1572864 | tf_op jit(solution)/shard_map/psum | solution.py:120
  866.0 1.5 copy-start.11
  882.1 15.9 %copy-start.16 = (f32[256,256]{1,0:T(8,128)S(1)}, f32[256,256]{1,0:T(8,128)}, u32[]{:S(2)}) copy-start(f32[256,256]{1,0:T(8,128)} %get-tuple-element.74) | copy-start | bytes 786436
  892.5 5.5 copy-start.17
  893.8 16.0 %collective-permute-start.6 = (f32[3,128,512]{2,1,0:T(8,128)}, f32[3,128,512]{2,1,0:T(8,128)}, u32[]{:S(2)}, u32[]{:S(2)}) collective-permute-start(f32[3,128,512]{2,1,0:T(8,128)} %get-tuple-element.111), channel_id=1, source_target_pairs={{0,8},{8,16},{16,24},{24,32},{32,40},{40,48},{48,56},{56,64},{64,7... | collective-permute-start | bytes 2359304 | tf_op jit(solution)/shard_map/ppermute | solution.py:14
  896.7 22.3 %collective-permute-start.7 = (f32[3,128,512]{2,1,0:T(8,128)}, f32[3,128,512]{2,1,0:T(8,128)}, u32[]{:S(2)}, u32[]{:S(2)}) collective-permute-start(f32[3,128,512]{2,1,0:T(8,128)} %get-tuple-element.110), channel_id=1, source_target_pairs={{8,0},{16,8},{24,16},{32,24},{40,32},{48,40},{56,48},{64,56},{72,6... | collective-permute-start | bytes 2359304 | tf_op jit(solution)/shard_map/ppermute | solution.py:17
  898.8 523.1 %all-reduce.15.cloned.1.call-start = ((), (), s32[]{:S(2)}) async-start(), calls=%async_computation.3 | async-start | bytes 3145728 | tf_op jit(solution)/shard_map/psum | solution.py:114
  912.0 411.8 %copy-start.7 = (f32[1,2,256,256]{3,2,1,0:T(8,128)S(1)}, f32[1,2,256,256]{3,2,1,0:T(8,128)}, u32[]{:S(2)}) copy-start(f32[1,2,256,256]{3,2,1,0:T(8,128)} %copy-done.6) | copy-start | bytes 1572868
  921.3 500.6 %copy-start.3 = (f32[1,256,512]{2,1,0:T(8,128)S(1)}, f32[1,256,512]{2,1,0:T(8,128)}, u32[]{:S(2)}) copy-start(f32[1,256,512]{2,1,0:T(8,128)} %copy-done.2) | copy-start | bytes 1572868
  921.4 500.6 %copy-start.5 = (f32[1,256,512]{2,1,0:T(8,128)S(1)}, f32[1,256,512]{2,1,0:T(8,128)}, u32[]{:S(2)}) copy-start(f32[1,256,512]{2,1,0:T(8,128)} %copy-done.4) | copy-start | bytes 1572868
Sparse Core Ops, SparseCore 0:
  51.4 90.2 all-reduce.8
  213.7 99.2 all-reduce.10
  316.4 413.6 all-reduce.18
  757.6 90.8 all-reduce.12
  899.0 423.7 all-reduce.16
  1325.3 96.6 all-reduce.14
where the time goes:
time: 1440 us; the launch traced here: 1430 us
  waiting for transfers between devices  1210 us (84%)
  matrix products  68.2 us (5%)
  local copies, waits for them, and re-layouts  62.8 us (4%)
  other arithmetic  32.7 us (2%)
  between operations  29.7 us (2%)
  starting transfers between devices  24.9 us (2%)
    psum x2, waiting for transfers between devices, shards(): step_total, coverage_total = lax.psum((step_stack, coverage), 'tile')  811 us
    psum x2, waiting for transfers between devices, shards(): summed = lax.psum(own_strip, 'mode')  195 us
    psum x2, waiting for transfers between devices, shards(): intensity = lax.psum(local_power, 'mode')  165 us
    dynamic_update_slice x4, local copies, waits for them, and re-layouts, place_add(): lax.dynamic_update_slice(target, current + placed, (zero_index, row_start...  42.4 us
    dot_general x16, matrix products, apply_right(): jnp.einsum('pab,bc->pac', target, matrix, precision=lax.Precision.HIGHEST)  34.4 us
    dot_general x16, matrix products, apply_left(): jnp.einsum('ab,pbc->pac', matrix, target, precision=lax.Precision.HIGHEST)  33.7 us
  transfers between devices with their start and end apart: 14, of which 12 were waited for; matrix products, arithmetic and copies ran while one was open for 1% of the time, Pallas kernels for 0%

commit v1 on v0

v1 whole, which is shorter than its diff:
```python
import math

import jax
import jax.numpy as jnp
import ml_dtypes
import numpy as np
from jax import lax
from jax.experimental import pallas as pl
from jax.experimental.pallas import tpu as pltpu
from jax.sharding import PartitionSpec as P

N = 256
HALF = 128
WIDTH = 512
OWN = 32
BATCHES = 2
F32 = jnp.float32
BF16 = jnp.bfloat16
MESH = pl.DeviceIdType.MESH


def split_tables():
    index = np.arange(N)
    angle = (np.outer(index, index) % N) * (2.0 * math.pi / N)
    cosine = np.cos(angle) / math.sqrt(N)
    sine = np.sin(angle) / math.sqrt(N)
    bf16 = ml_dtypes.bfloat16

    def parts(table):
        high = table.astype(np.float32).astype(bf16)
        low = (table - high.astype(np.float64)).astype(np.float32).astype(bf16)
        return high, low

    ch, cl = parts(cosine)
    sh, sl = parts(sine)
    high = np.concatenate([ch, sh], axis=1)
    low = np.concatenate([cl, sl], axis=1)
    right = np.concatenate([high, low, high], axis=0)
    left = np.concatenate(
        [np.concatenate([ch, ch, cl], axis=1), np.concatenate([sh, sh, sl], axis=1)], axis=0
    )
    left = left.reshape(2, 4, 64, 3 * N).transpose(1, 0, 2, 3).reshape(4, 128, 3 * N)
    return right, left


def halves(value):
    high = value.astype(BF16)
    low = (value - high.astype(F32)).astype(BF16)
    return high, low


def dot(a, b):
    return jnp.dot(a, b, preferred_element_type=F32)


def iota(shape, dim):
    return lax.broadcasted_iota(jnp.int32, shape, dim)


def scratch_plan():
    plan = {}
    for b in range(BATCHES):
        plan[f"halo{b}"] = pltpu.VMEM((2, OWN, WIDTH), F32)
        plan[f"patch{b}"] = pltpu.VMEM((2, N, N), F32)
        plan[f"pout{b}"] = pltpu.VMEM((2, 2, OWN, N), F32)
        plan[f"probes{b}"] = pltpu.VMEM((2, 3, N, N), F32)
        plan[f"power{b}"] = pltpu.VMEM((8, 8, N), F32)
        plan[f"inten{b}"] = pltpu.VMEM((N, N), F32)
        plan[f"irecv{b}"] = pltpu.VMEM((3, 64, N), F32)
        plan[f"factor{b}"] = pltpu.VMEM((N, N), F32)
        plan[f"grad{b}"] = pltpu.VMEM((2, N, N), F32)
        plan[f"grecv{b}"] = pltpu.VMEM((7, 2, OWN, N), F32)
        plan[f"gown{b}"] = pltpu.VMEM((2, 2, OWN, N), F32)
        plan[f"gnear{b}"] = pltpu.VMEM((2, 2, OWN, N), F32)
        plan[f"objnew{b}"] = pltpu.VMEM((2, OWN, WIDTH), F32)
        plan[f"dstep{b}"] = pltpu.VMEM((2, 2, N, N), F32)
        plan[f"dsib{b}"] = pltpu.VMEM((2, N, N), F32)
        plan[f"cov{b}"] = pltpu.VMEM((1, N, N), F32)
        plan[f"csib{b}"] = pltpu.VMEM((1, N, N), F32)
        for name, parts in (("p", 2), ("c", 1)):
            plan[f"{name}full{b}"] = pltpu.VMEM((parts, N, N), F32)
            plan[f"{name}y{b}"] = pltpu.VMEM((3, parts, 64, N), F32)
            plan[f"{name}ya{b}"] = pltpu.VMEM((parts, 64, N), F32)
            plan[f"{name}x{b}"] = pltpu.VMEM((3, parts, 16, N), F32)
            plan[f"{name}xa{b}"] = pltpu.VMEM((parts, 16, N), F32)
            plan[f"{name}z{b}"] = pltpu.VMEM((parts, 8, N), F32)
    plan["where_own"] = pltpu.VMEM((8, N), jnp.int32)
    plan["where_near"] = pltpu.VMEM((8, N), jnp.int32)
    plan["ofield"] = pltpu.VMEM((2, N, N), F32)
    plan["far"] = pltpu.VMEM((2, 2, N, N), F32)
    plan["stage"] = pltpu.VMEM((2, 3 * N, 2 * N), BF16)
    plan["illum"] = pltpu.VMEM((OWN, WIDTH), F32)
    return plan


COPIES = 136


def kernel(names, pos, obj, probe, measured, rw, lw, out_obj, out_probe, *scratch):
    buf = dict(zip(names, scratch))
    ssem, rsem = scratch[len(names)], scratch[len(names) + 1]
    t = lax.axis_index("tile")
    m = lax.axis_index("mode")
    x, zh, y = t // 8, (t // 4) % 2, t % 4
    z, c = m // 2, m % 2
    sibling = m + 1 - 2 * c
    side = 1 - 2 * (m // 4)
    t_plus = lax.rem(t + side + 32, 32)
    t_minus = lax.rem(t - side + 32, 32)
    t_pair = t + 4 - 8 * zh
    own_row = pl.multiple_of(OWN * m, OWN)
    y_row = pl.multiple_of(64 * y, 64)
    x_sub = pl.multiple_of(16 * x, 16)
    x_row = pl.multiple_of(64 * y + 16 * x, 16)
    z_sub = pl.multiple_of(8 * zh, 8)
    z_other = pl.multiple_of(8 - 8 * zh, 8)
    z_row = pl.multiple_of(64 * y + 16 * x + 8 * zh, 8)
    i_row = pl.multiple_of(64 * z, 64)
    sent = []

    def send(src, dst, tile, mode):
        index = len(sent)
        copy = pltpu.make_async_remote_copy(
            src_ref=src,
            dst_ref=dst,
            send_sem=ssem.at[index],
            recv_sem=rsem.at[index],
            device_id=(tile, mode),
            device_id_type=MESH,
        )
        copy.start()
        sent.append(copy)
        return copy

    def arrived(copies):
        for copy in copies:
            copy.wait_recv()

    def y_tile(k):
        other = lax.rem(y + k, 4)
        return other, t - y + other

    def x_tile(k):
        other = lax.rem(x + k, 4)
        return other, t - 8 * x + 8 * other

    barrier = pltpu.get_barrier_semaphore()
    partners = [(t, lax.rem(m + k, 8)) for k in range(1, 8)]
    partners += [(y_tile(k)[1], m) for k in range(1, 4)]
    partners += [(x_tile(k)[1], m) for k in range(1, 4)]
    partners += [(t_pair, m), (t_plus, m), (t_minus, m)]
    for partner in partners:
        pl.semaphore_signal(barrier, inc=1, device_id=partner, device_id_type=MESH)

    for b in range(BATCHES):
        for j in range(2):
            core = c if j == 0 else 1 - c
            row = pos[b, core, 0] - N * t
            column = pos[b, core, 1]
            buf["where_own"][4 * b + 2 * j : 4 * b + 2 * j + 1, :] = jnp.full((1, N), row, jnp.int32)
            buf["where_own"][4 * b + 2 * j + 1 : 4 * b + 2 * j + 2, :] = jnp.full(
                (1, N), column, jnp.int32
            )
    for part in range(2):
        buf["probes0"][0, part] = probe[0, part]
    pl.semaphore_wait(barrier, len(partners))

    def place(ref, b, j):
        return ref[4 * b + 2 * j : 4 * b + 2 * j + 1, :], ref[4 * b + 2 * j + 1 : 4 * b + 2 * j + 2, :]

    class Reduce:
        def __init__(self, name, b):
            self.full, self.y, self.ya, self.x, self.xa, self.z = (
                buf[f"{name}{part}{b}"] for part in ("full", "y", "ya", "x", "xa", "z")
            )

        def start_y(self):
            self.copies = []
            for k in range(1, 4):
                other, tile = y_tile(k)
                rows = pl.ds(pl.multiple_of(64 * other, 64), 64)
                self.copies.append(send(self.full.at[:, rows], self.y.at[k - 1], tile, m))

        def start_x(self):
            arrived(self.copies)
            self.ya[...] = self.full[:, pl.ds(y_row, 64)] + self.y[0] + self.y[1] + self.y[2]
            self.copies = []
            for k in range(1, 4):
                other, tile = x_tile(k)
                rows = pl.ds(pl.multiple_of(16 * other, 16), 16)
                self.copies.append(send(self.ya.at[:, rows], self.x.at[k - 1], tile, m))

        def start_z(self):
            arrived(self.copies)
            self.xa[...] = self.ya[:, pl.ds(x_sub, 16)] + self.x[0] + self.x[1] + self.x[2]
            self.copies = [send(self.xa.at[:, pl.ds(z_other, 8)], self.z, t_pair, m)]

        def finish(self):
            arrived(self.copies)
            return self.xa[:, pl.ds(z_sub, 8)] + self.z[...]

    class Gather:
        def __init__(self, view):
            self.view = view

        def start_z(self):
            part = self.view(pl.ds(z_row, 8))
            self.copies = [send(part, part, t_pair, m)]

        def start_x(self):
            arrived(self.copies)
            part = self.view(pl.ds(x_row, 16))
            self.copies = [send(part, part, x_tile(k)[1], m) for k in range(1, 4)]

        def start_y(self):
            arrived(self.copies)
            part = self.view(pl.ds(y_row, 64))
            self.copies = [send(part, part, y_tile(k)[1], m) for k in range(1, 4)]

        def finish(self):
            arrived(self.copies)

    def send_power(b, real, imag):
        power = buf[f"power{b}"]
        power[0] = real * real + imag * imag
        return [
            send(power.at[0], power.at[k], t, lax.rem(m + k, 8)) for k in range(1, 8)
        ]

    def sum_power(b, copies):
        arrived(copies)
        power = buf[f"power{b}"]
        total = power[0]
        for k in range(1, 8):
            total = total + power[k]
        return total

    def send_patches(b, field, field_rows):
        halo, out, patch = buf[f"halo{b}"], buf[f"pout{b}"], buf[f"patch{b}"]
        rows = own_row + iota((OWN, N), 0)
        columns = iota((OWN, N), 1)
        for j in range(2):
            row, column = place(buf["where_own"], b, j)
            ahead = rows - row
            inside = (ahead >= 0) & (ahead < N)
            first = columns >= column
            for part in range(2):
                low = jnp.where(inside, field[part, field_rows, :N], halo[part, :, :N])
                high = jnp.where(inside, field[part, field_rows, N:], halo[part, :, N:])
                out[j, part] = jnp.where(first, low, high)
        copies = []
        for k in range(1, 8):
            copies.append(
                send(out.at[k % 2], patch.at[:, pl.ds(own_row, OWN)], t, lax.rem(m + k, 8))
            )
        patch[:, pl.ds(own_row, OWN)] = out[0]
        return copies

    def shifted(real, imag, row, column):
        i0, i1 = iota((N, N), 0), iota((N, N), 1)
        pick = (((i0 + row) & (N - 1)) == i1).astype(F32).astype(BF16)
        high, low = halves(jnp.concatenate([real, imag], axis=1))
        moved = dot(jnp.concatenate([pick, pick], axis=1), jnp.concatenate([high, low], axis=0))
        pick = (((i1 + column) & (N - 1)) == i0).astype(F32).astype(BF16)
        high, low = halves(jnp.concatenate([moved[:, :N], moved[:, N:]], axis=0))
        moved = dot(jnp.concatenate([high, low], axis=1), jnp.concatenate([pick, pick], axis=0))
        return moved[:N], moved[N:]

    def chunk_rows(q):
        return pl.ds(pl.multiple_of(q * 64, 64), 64)

    stage = buf["stage"]

    def right_stage(mode, q, real, imag, sign):
        high, low = halves(jnp.concatenate([real, imag], axis=0))
        product = dot(jnp.concatenate([high, high, low], axis=1), rw[...])
        out_real = product[:64, :N] + sign * product[64:, N:]
        out_imag = product[64:, :N] - sign * product[:64, N:]
        high, low = halves(jnp.concatenate([out_real, out_imag], axis=1))
        stage[mode, pl.ds(pl.multiple_of(q * 64, 64), 64), :] = high
        stage[mode, pl.ds(pl.multiple_of(N + q * 64, 64), 64), :] = low
        stage[mode, pl.ds(pl.multiple_of(2 * N + q * 64, 64), 64), :] = high

    def left_stage(mode, q, sign):
        product = dot(lw[q], stage[mode])
        return (
            product[:64, :N] + sign * product[64:, N:],
            product[:64, N:] - sign * product[64:, :N],
        )

    far, ofield = buf["far"], buf["ofield"]

    def forward(b):
        probes, inten = buf[f"probes{b}"], buf[f"inten{b}"]

        def first(q, carry):
            rows = chunk_rows(q)
            o_real, o_imag = ofield[0, rows, :], ofield[1, rows, :]
            for mode in range(2):
                p_real, p_imag = probes[mode, 0, rows, :], probes[mode, 1, rows, :]
                right_stage(
                    mode,
                    q,
                    p_real * o_real - p_imag * o_imag,
                    p_real * o_imag + p_imag * o_real,
                    1.0,
                )
            return carry

        lax.fori_loop(0, 4, first, 0)

        def second(q, carry):
            rows = chunk_rows(q)
            total = None
            for mode in range(2):
                f_real, f_imag = left_stage(mode, q, 1.0)
                far[mode, 0, rows, :] = f_real
                far[mode, 1, rows, :] = f_imag
                power = f_real * f_real + f_imag * f_imag
                total = power if total is None else total + power
            inten[rows, :] = total
            return carry

        lax.fori_loop(0, 4, second, 0)

    def inverse(b):
        probes, factor = buf[f"probes{b}"], buf[f"factor{b}"]
        grad, dstep = buf[f"grad{b}"], buf[f"dstep{b}"]

        def first(q, carry):
            rows = chunk_rows(q)
            scale = factor[rows, :]
            for mode in range(2):
                right_stage(mode, q, scale * far[mode, 0, rows, :], scale * far[mode, 1, rows, :], -1.0)
            return carry

        lax.fori_loop(0, 4, first, 0)

        def second(q, carry):
            rows = chunk_rows(q)
            o_real, o_imag = ofield[0, rows, :], ofield[1, rows, :]
            g_real = jnp.zeros((64, N), F32)
            g_imag = jnp.zeros((64, N), F32)
            for mode in range(2):
                c_real, c_imag = left_stage(mode, q, -1.0)
                p_real, p_imag = probes[mode, 0, rows, :], probes[mode, 1, rows, :]
                g_real = g_real + p_real * c_real + p_imag * c_imag
                g_imag = g_imag + p_real * c_imag - p_imag * c_real
                dstep[mode, 0, rows, :] = o_real * c_real + o_imag * c_imag
                dstep[mode, 1, rows, :] = o_real * c_imag - o_imag * c_real
            grad[0, rows, :] = g_real
            grad[1, rows, :] = g_imag
            return carry

        lax.fori_loop(0, 4, second, 0)
        row, column = place(buf["where_own"], b, 0)
        grad[0], grad[1] = shifted(grad[0], grad[1], -row, -column)

    def masks(b):
        rows = own_row + iota((OWN, N), 0)
        columns = iota((OWN, N), 1)
        found = []
        for ref, near in ((buf["where_own"], False), (buf["where_near"], True)):
            for j in range(2):
                row, column = place(ref, b, j)
                ahead = rows - row
                inside = (ahead >= 0) & (ahead < N)
                if near:
                    inside = jnp.logical_not(inside)
                first = columns >= column
                found.append((inside & first, inside & jnp.logical_not(first)))
        return found

    def illumination(b):
        high, low = halves(buf[f"probes{b}"][0, 2])
        power = jnp.concatenate([high, low], axis=0)
        rows = own_row + iota((OWN, N), 0)
        lanes = iota((OWN, N), 1)
        places = [
            place(ref, b, j) for ref in (buf["where_own"], buf["where_near"]) for j in range(2)
        ]
        picks = []
        for row, _ in places:
            pick = (((rows - row) & (N - 1)) == lanes).astype(F32).astype(BF16)
            picks.append(jnp.concatenate([pick, pick], axis=1))
        taken = dot(jnp.concatenate(picks, axis=0), power)
        i0, i1 = iota((N, N), 0), iota((N, N), 1)
        left = jnp.zeros((OWN, N), F32)
        right = jnp.zeros((OWN, N), F32)
        for index, ((_, column), (in_left, in_right)) in enumerate(zip(places, masks(b))):
            pick = (((i1 - column) & (N - 1)) == i0).astype(F32).astype(BF16)
            high, low = halves(taken[OWN * index : OWN * (index + 1)])
            moved = dot(
                jnp.concatenate([high, low], axis=1), jnp.concatenate([pick, pick], axis=0)
            )
            left = left + jnp.where(in_left, moved, 0.0)
            right = right + jnp.where(in_right, moved, 0.0)
        buf["illum"][:, :N] = left
        buf["illum"][:, N:] = right

    def update_object(b, field, field_rows):
        own, near, new = buf[f"gown{b}"], buf[f"gnear{b}"], buf[f"objnew{b}"]
        found = masks(b)
        for part in range(2):
            steps = [own[0, part], own[1, part], near[0, part], near[1, part]]
            for side_index, columns in ((0, slice(0, N)), (1, slice(N, WIDTH))):
                total = jnp.zeros((OWN, N), F32)
                for step, mask in zip(steps, found):
                    total = total + jnp.where(mask[side_index], step, 0.0)
                new[part, :, columns] = field[part, field_rows, columns] + total / (
                    buf["illum"][:, columns] + 1.0
                )

    halo_copy = send(obj.at[:, pl.ds(own_row, OWN)], buf["halo0"], t_minus, m)
    probe_copy = send(buf["probes0"].at[0, pl.ds(0, 2)], buf["probes0"].at[1, pl.ds(0, 2)], t, sibling)
    where_copy = send(buf["where_own"], buf["where_near"], t_plus, m)
    power_copies = send_power(0, probe[0, 0, pl.ds(z_row, 8)], probe[0, 1, pl.ds(z_row, 8)])
    arrived([halo_copy])
    patch_copies = send_patches(0, obj, pl.ds(own_row, OWN))
    buf["probes0"][0, 2, pl.ds(z_row, 8)] = sum_power(0, power_copies)
    power_gather = Gather(lambda rows: buf["probes0"].at[0, 2, rows])
    power_gather.start_z()
    arrived([where_copy])
    probe_gather = None

    for b in range(BATCHES):
        last = b == BATCHES - 1
        if b == 0:
            field, field_rows = obj, pl.ds(own_row, OWN)
        else:
            field, field_rows = buf[f"objnew{b - 1}"], slice(0, OWN)
        arrived(patch_copies)
        row, column = place(buf["where_own"], b, 0)
        patch = buf[f"patch{b}"]
        ofield[0], ofield[1] = shifted(patch[0], patch[1], row, column)
        cover = buf[f"cov{b}"]
        cover[0] = ofield[0] * ofield[0] + ofield[1] * ofield[1]
        cover_copy = send(cover, buf[f"csib{b}"], t, sibling)
        arrived([probe_copy])
        forward(b)
        inten, irecv, factor = buf[f"inten{b}"], buf[f"irecv{b}"], buf[f"factor{b}"]
        copies = []
        for k in range(1, 4):
            other = lax.rem(z + k, 4)
            rows = pl.ds(pl.multiple_of(64 * other, 64), 64)
            copies.append(send(inten.at[rows], irecv.at[k - 1], t, 2 * other + c))
        if b == 0:
            power_gather.start_x()
        arrived([cover_copy])
        buf[f"cfull{b}"][...] = cover[...] + buf[f"csib{b}"][...]
        cover_sum = Reduce("c", b)
        cover_sum.start_y()
        arrived(copies)
        own_rows = pl.ds(i_row, 64)
        total = inten[own_rows, :] + irecv[0] + irecv[1] + irecv[2]
        factor[own_rows, :] = jnp.sqrt((measured[b, c, own_rows, :] + 1.0) / (total + 1.0)) - 1.0
        copies = []
        for k in range(1, 4):
            other = lax.rem(z + k, 4)
            copies.append(send(factor.at[own_rows], factor.at[own_rows], t, 2 * other + c))
        if b == 0:
            power_gather.start_y()
        cover_sum.start_x()
        arrived(copies)
        inverse(b)
        grad, grecv, dstep = buf[f"grad{b}"], buf[f"grecv{b}"], buf[f"dstep{b}"]
        copies = []
        for k in range(1, 8):
            other = lax.rem(m + k, 8)
            rows = pl.ds(pl.multiple_of(OWN * other, OWN), OWN)
            copies.append(send(grad.at[:, rows], grecv.at[k - 1], t, other))
        step_copy = send(dstep.at[1], buf[f"dsib{b}"], t, sibling)
        cover_sum.start_z()
        if b == 0:
            power_gather.finish()
        arrived([step_copy])
        buf[f"pfull{b}"][...] = dstep[0] + buf[f"dsib{b}"][...]
        probe_sum = Reduce("p", b)
        probe_sum.start_y()
        illumination(b)
        arrived(copies)
        gown = buf[f"gown{b}"]
        gown[0] = grad[:, pl.ds(own_row, OWN)] + grecv[1] + grecv[3] + grecv[5]
        gown[1] = grecv[0] + grecv[2] + grecv[4] + grecv[6]
        near_copy = send(gown, buf[f"gnear{b}"], t_plus, m)
        probe_sum.start_x()
        arrived([near_copy])
        update_object(b, field, field_rows)
        new = buf[f"objnew{b}"]
        if last:
            rows = pl.ds(own_row, OWN)
            final_copies = [
                send(new, out_obj.at[:, rows], t, lax.rem(m + k, 8)) for k in range(1, 8)
            ]
            out_obj[:, rows] = new[...]
        else:
            halo_copy = send(new, buf[f"halo{b + 1}"], t_minus, m)
        probe_sum.start_z()
        coverage = cover_sum.finish()[0]
        step = probe_sum.finish()
        probes = buf[f"probes{b}"]
        rows = pl.ds(z_row, 8)
        updated = [probes[0, part, rows, :] + step[part] / (coverage + 1.0) for part in range(2)]
        if last:
            for part in range(2):
                out_probe[0, part, rows, :] = updated[part]
            gather = Gather(lambda rows: out_probe.at[0, :, rows])
            gather.start_z()
            gather.start_x()
            gather.start_y()
            arrived(final_copies)
            gather.finish()
        else:
            following = buf[f"probes{b + 1}"]
            for part in range(2):
                following[0, part, rows, :] = updated[part]
            power_copies = send_power(b + 1, updated[0], updated[1])
            arrived([halo_copy])
            patch_copies = send_patches(b + 1, new, slice(0, OWN))
            following[0, 2, rows, :] = sum_power(b + 1, power_copies)
            gather = Gather(lambda rows: following.at[0, :, rows])
            gather.start_z()
            gather.start_x()
            gather.start_y()
            gather.finish()
            probe_copy = send(following.at[0, pl.ds(0, 2)], following.at[1, pl.ds(0, 2)], t, sibling)

    for copy in sent:
        copy.wait_send()


def shards(object_field, probe, positions, measured):
    right, left = split_tables()
    plan = scratch_plan()
    names = list(plan)

    def body(*refs):
        kernel(names, *refs)

    vmem = pl.BlockSpec(memory_space=pltpu.VMEM)
    return pl.pallas_call(
        body,
        name="refine",
        out_shape=(
            jax.ShapeDtypeStruct(object_field.shape, F32),
            jax.ShapeDtypeStruct(probe.shape, F32),
        ),
        in_specs=[pl.BlockSpec(memory_space=pltpu.SMEM)] + [vmem] * 5,
        out_specs=(vmem, vmem),
        scratch_shapes=list(plan.values())
        + [pltpu.SemaphoreType.DMA((COPIES,)), pltpu.SemaphoreType.DMA((COPIES,))],
        compiler_params=pltpu.CompilerParams(
            collective_id=0, has_side_effects=True, vmem_limit_bytes=56 * 1024 * 1024
        ),
    )(positions, object_field, probe, measured, jnp.asarray(right), jnp.asarray(left))


def solution(mesh):
    in_specs = (
        P(None, "tile", None),
        P("mode", None, None, None),
        P(None, "tile", None),
        P(None, "tile", None, None),
    )
    out_specs = (P(None, "tile", None), P("mode", None, None, None))
    return jax.shard_map(shards, mesh=mesh, in_specs=in_specs, out_specs=out_specs, check_vma=False)
```

time: 1440 us -> 191 us (0.13)
  waiting for transfers between devices: 1210 us -> 0 us
  Pallas kernels: 0 us -> 186 us
  matrix products: 68.2 us -> 0 us
  local copies, waits for them, and re-layouts: 62.8 us -> 3.12 us
  other arithmetic: 32.7 us -> 0 us
  between operations: 29.7 us -> 0.65 us
  starting transfers between devices: 24.9 us -> 0 us
    psum x6 -> x0, waiting for transfers between devices: 1170 us -> none  [the longest x2 811 us: shards(): step_total, coverage_total = lax.psum((step_stack, coverage), 'tile')]
    pallas_call x0 -> x1, Pallas kernels: none -> 186 us  [shards(): pl.pallas_call(body, name='refine', out_shape=(jax.ShapeDtypeStruct(objec...]
    dot_general x32 -> x0, matrix products: 68.2 us -> none  [the longest x16 34.4 us: apply_right(): jnp.einsum('pab,bc->pac', target, matrix, precision=lax.Precision.HIGHEST)]
    dynamic_update_slice x4 -> x0, local copies, waits for them, and re-layouts: 42.4 us -> none  [place_add(): lax.dynamic_update_slice(target, current + placed, (zero_index, row_start...]
    ppermute x8 -> x0, waiting for transfers between devices: 41.7 us -> none  [the longest x4 28.7 us: padded(): lax.ppermute(lax.slice_in_dim(block, block.shape[dim] - width, None, axis...]
    ppermute x8 -> x0, starting transfers between devices: 24.6 us -> none  [the longest x4 19.5 us: padded(): lax.ppermute(lax.slice_in_dim(block, block.shape[dim] - width, None, axis...]
  transfers between devices with their start and end apart: 14 -> 0, of which waited for: 12 -> 0; matrix products, arithmetic and copies ran while one was open for 1% -> 0% of each run, Pallas kernels for 0% -> 0%
where the time goes in v1:
time: 191 us; the launch traced here: 190 us
  Pallas kernels  186 us (97%)
  local copies, waits for them, and re-layouts  3.12 us (2%)
    pallas_call x1, Pallas kernels, shards(): pl.pallas_call(body, name='refine', out_shape=(jax.ShapeDtypeStruct(objec...  186 us

profile of v1, /device:TPU:1, one launch (start us, length us, event | category | flops | bytes accessed | tf_op | source)
XLA Modules:
  0.0 190.0 jit_solution(2558158138646126804)
XLA Ops:
  0.6 186.3 %refine.1 = (f32[2,256,512]{2,1,0:T(8,128)}, f32[1,2,256,256]{3,2,1,0:T(8,128)}) custom-call(s32[2,2,2]{2,1,0:T(2,128)} %refs_0_.1, f32[2,256,512]{2,1,0:T(8,128)} %refs_1_.1, f32[1,2,256,256]{3,2,1,0:T(8,128)} %refs_2_.1, f32[2,2,256,256]{3,2,1,0:T(8,128)} %refs_3_.1, bf16[768,512]{1,0:T(8,128)(2,1)} %constant.4.clone.refs_4_, ...), custom_call_target="tpu_custom_call" | custom-call | tf_op jit(solution)/shard_map/refine/pallas_call | solution.py:541
  186.9 0.0 copy-start
  186.9 2.3 %copy.10 = f32[2,256,512]{2,1,0:T(8,128)} copy(f32[2,256,512]{2,1,0:T(8,128)} %get-tuple-element.4) | data formatting | bytes 2097152
  189.3 0.0 copy-done
  189.3 0.8 copy.11
Async XLA Ops:
  186.9 2.3 %copy-start = (f32[1,2,256,256]{3,2,1,0:T(8,128)S(1)}, f32[1,2,256,256]{3,2,1,0:T(8,128)}, u32[]{:S(2)}) copy-start(f32[1,2,256,256]{3,2,1,0:T(8,128)} %get-tuple-element.5) | copy-start | bytes 1572868

commit v2 on v1

v2 whole, which is shorter than its diff:
```python
import math

import jax
import jax.numpy as jnp
import ml_dtypes
import numpy as np
from jax import lax
from jax.experimental import pallas as pl
from jax.experimental.pallas import tpu as pltpu
from jax.sharding import PartitionSpec as P

N = 256
HALF = 128
WIDTH = 512
OWN = 32
BATCHES = 2
F32 = jnp.float32
BF16 = jnp.bfloat16
MESH = pl.DeviceIdType.MESH


def split_tables():
    index = np.arange(N)
    angle = (np.outer(index, index) % N) * (2.0 * math.pi / N)
    cosine = np.cos(angle) / math.sqrt(N)
    sine = np.sin(angle) / math.sqrt(N)
    bf16 = ml_dtypes.bfloat16

    def parts(table):
        high = table.astype(np.float32).astype(bf16)
        low = (table - high.astype(np.float64)).astype(np.float32).astype(bf16)
        return high, low

    ch, cl = parts(cosine)
    sh, sl = parts(sine)
    high = np.concatenate([ch, sh], axis=1)
    low = np.concatenate([cl, sl], axis=1)
    right = np.concatenate([high, low, high], axis=0)
    left = np.concatenate(
        [np.concatenate([ch, ch, cl], axis=1), np.concatenate([sh, sh, sl], axis=1)], axis=0
    )
    left = left.reshape(2, 4, 64, 3 * N).transpose(1, 0, 2, 3).reshape(4, 128, 3 * N)
    return right, left


def halves(value):
    high = value.astype(BF16)
    low = (value - high.astype(F32)).astype(BF16)
    return high, low


def dot(a, b):
    return jnp.dot(a, b, preferred_element_type=F32)


def iota(shape, dim):
    return lax.broadcasted_iota(jnp.int32, shape, dim)


def reduce_plan(parts):
    return dict(
        full=pltpu.VMEM((parts, N, N), F32),
        one=pltpu.VMEM((2, 3, parts, 32, N), F32),
        onesum=pltpu.VMEM((2, parts, 32, N), F32),
        two=pltpu.VMEM((2, 3, parts, 8, N), F32),
        twosum=pltpu.VMEM((2, parts, 8, N), F32),
        pair=pltpu.VMEM((2, parts, 8, N), F32),
    )


def batch_plan():
    return dict(
        halo=pltpu.VMEM((2, OWN, WIDTH), F32),
        patch=pltpu.VMEM((2, N, N), F32),
        pout=pltpu.VMEM((2, 2, OWN, N), F32),
        probes=pltpu.VMEM((2, 3, N, N), F32),
        power=pltpu.VMEM((8, 2, 8, N), F32),
        inten=pltpu.VMEM((N, N), F32),
        irecv=pltpu.VMEM((3, 64, N), F32),
        factor=pltpu.VMEM((N, N), F32),
        grad=pltpu.VMEM((2, N, N), F32),
        grecv=pltpu.VMEM((7, 2, OWN, N), F32),
        gown=pltpu.VMEM((2, 2, OWN, N), F32),
        gminus=pltpu.VMEM((2, 2, OWN, N), F32),
        gplus=pltpu.VMEM((2, 2, OWN, N), F32),
        objnew=pltpu.VMEM((2, OWN, WIDTH), F32),
        dstep=pltpu.VMEM((2, 2, N, N), F32),
        dsib=pltpu.VMEM((2, N, N), F32),
        cov=pltpu.VMEM((1, N, N), F32),
        csib=pltpu.VMEM((1, N, N), F32),
        probe_sum=reduce_plan(2),
        cover_sum=reduce_plan(1),
    )


def scratch_plan():
    common = dict(
        edge_plus=pltpu.VMEM((2, 16, WIDTH), F32),
        edge_minus=pltpu.VMEM((2, 16, WIDTH), F32),
        edge_out=pltpu.VMEM((2, 2, 16, N), F32),
        edge_rows=pltpu.VMEM((2, HALF, N), F32),
        observed=pltpu.VMEM((2, N, N), F32),
        rtable=pltpu.VMEM((3 * N, 2 * N), BF16),
        ltable=pltpu.VMEM((4, 128, 3 * N), BF16),
        where_own=pltpu.VMEM((8, N), jnp.int32),
        where_minus=pltpu.VMEM((8, N), jnp.int32),
        where_plus=pltpu.VMEM((8, N), jnp.int32),
        rolled=pltpu.VMEM((2, 2, N, N), F32),
        far=pltpu.VMEM((2, 2, N, N), F32),
        stage=pltpu.VMEM((2, 3 * N, 2 * N), BF16),
        illum=pltpu.VMEM((2, OWN, WIDTH), F32),
    )
    return [common] + [batch_plan() for _ in range(BATCHES)]


class Box:
    def __init__(self, entries):
        for name, entry in entries.items():
            setattr(self, name, Box(entry) if isinstance(entry, dict) else entry)


COPIES = 200


def kernel(tree, pos, obj, probe, measured, rtable, ltable, out_obj, out_probe, *scratch):
    ssem, rsem, lsem = scratch[-3:]
    com, *mem = [Box(entries) for entries in jax.tree.unflatten(tree, scratch[:-3])]
    t = lax.axis_index("tile")
    m = lax.axis_index("mode")
    x, zh, y = t // 8, (t // 4) % 2, t % 4
    z, c = m // 2, m % 2
    sibling = m + 1 - 2 * c
    side = 1 - 2 * (m // 4)
    t_plus = lax.rem(t + side + 32, 32)
    t_minus = lax.rem(t - side + 32, 32)
    t_pair = t + 4 - 8 * zh
    own_row = pl.multiple_of(OWN * m, OWN)
    i_row = pl.multiple_of(64 * z, 64)
    sent = []

    def send(src, dst, tile, mode):
        index = len(sent)
        copy = pltpu.make_async_remote_copy(
            src_ref=src,
            dst_ref=dst,
            send_sem=ssem.at[index],
            recv_sem=rsem.at[index],
            device_id=(tile, mode),
            device_id_type=MESH,
        )
        copy.start()
        sent.append(copy)
        return copy

    def arrived(copies):
        for copy in copies:
            copy.wait_recv()

    def y_tile(k):
        other = lax.rem(y + k, 4)
        return other, t - y + other

    def x_tile(k):
        other = lax.rem(x + k, 4)
        return other, t - 8 * x + 8 * other

    barrier = pltpu.get_barrier_semaphore()
    rw, lw, observed = com.rtable, com.ltable, com.observed
    loads = [
        pltpu.make_async_copy(rtable, rw, lsem.at[0]),
        pltpu.make_async_copy(ltable, lw, lsem.at[1]),
        pltpu.make_async_copy(measured.at[0, c], observed.at[0], lsem.at[2]),
        pltpu.make_async_copy(measured.at[1, c], observed.at[1], lsem.at[3]),
    ]
    partners = [(t, lax.rem(m + k, 8)) for k in range(1, 8)]
    partners += [(y_tile(k)[1], m) for k in range(1, 4)]
    partners += [(x_tile(k)[1], m) for k in range(1, 4)]
    partners += [(t_pair, m), (t_plus, m), (t_minus, m)]
    for partner in partners:
        pl.semaphore_signal(barrier, inc=1, device_id=partner, device_id_type=MESH)
    for load in loads:
        load.start()

    for b in range(BATCHES):
        for j in range(2):
            core = c if j == 0 else 1 - c
            row = pos[b, core, 0] - N * t
            column = pos[b, core, 1]
            com.where_own[4 * b + 2 * j : 4 * b + 2 * j + 1, :] = jnp.full((1, N), row, jnp.int32)
            com.where_own[4 * b + 2 * j + 1 : 4 * b + 2 * j + 2, :] = jnp.full(
                (1, N), column, jnp.int32
            )
    for part in range(2):
        mem[0].probes[0, part] = probe[0, part]
    pl.semaphore_wait(barrier, len(partners))

    def place(ref, b, j):
        return ref[4 * b + 2 * j : 4 * b + 2 * j + 1, :], ref[4 * b + 2 * j + 1 : 4 * b + 2 * j + 2, :]

    def whole(part, other):
        return pl.ds(pl.multiple_of(HALF * part + 32 * other, 32), 32)

    def piece(other):
        return pl.ds(pl.multiple_of(8 * other, 8), 8)

    lines = ((y_tile, x_tile), (x_tile, y_tile))
    spots = ((y, x), (x, y))
    held = [
        pl.ds(pl.multiple_of(HALF * part + 32 * spots[part][0] + 8 * spots[part][1], 8), 8)
        for part in range(2)
    ]

    class Reduce:
        def __init__(self, box):
            self.full, self.one, self.onesum = box.full, box.one, box.onesum
            self.two, self.twosum, self.pair = box.two, box.twosum, box.pair

        def start_one(self):
            self.copies = [[], []]
            for k in range(1, 4):
                for part in range(2):
                    other, tile = lines[part][0](k)
                    self.copies[part].append(
                        send(self.full.at[:, whole(part, other)], self.one.at[part, k - 1], tile, m)
                    )

        def start_two(self):
            after = [[], []]
            for part in range(2):
                arrived(self.copies[part])
                self.onesum[part] = (
                    self.full[:, whole(part, spots[part][0])]
                    + self.one[part, 0]
                    + self.one[part, 1]
                    + self.one[part, 2]
                )
                for k in range(1, 4):
                    other, tile = lines[part][1](k)
                    after[part].append(
                        send(
                            self.onesum.at[part, :, piece(other)], self.two.at[part, k - 1], tile, m
                        )
                    )
            self.copies = after

        def start_pair(self):
            for part in range(2):
                arrived(self.copies[part])
                self.twosum[part] = (
                    self.onesum[part, :, piece(spots[part][1])]
                    + self.two[part, 0]
                    + self.two[part, 1]
                    + self.two[part, 2]
                )
            self.copies = [send(self.twosum, self.pair, t_pair, m)]

        def finish(self):
            arrived(self.copies)
            return [self.twosum[part] + self.pair[part] for part in range(2)]

    class Gather:
        def __init__(self, view):
            self.view = view

        def start_one(self):
            self.copies = [[], []]
            for k in range(1, 4):
                for part in range(2):
                    rows = self.view(held[part])
                    self.copies[part].append(send(rows, rows, lines[part][1](k)[1], m))

        def start_two(self):
            after = [[], []]
            for part in range(2):
                arrived(self.copies[part])
                rows = self.view(whole(part, spots[part][0]))
                for k in range(1, 4):
                    after[part].append(send(rows, rows, lines[part][0](k)[1], m))
            self.copies = after

        def finish(self):
            for part in range(2):
                arrived(self.copies[part])

    def send_power(b, values):
        power = mem[b].power
        for part, (real, imag) in enumerate(values):
            power[0, part] = real * real + imag * imag
        return [send(power.at[0], power.at[k], t, lax.rem(m + k, 8)) for k in range(1, 8)]

    def sum_power(b, copies):
        arrived(copies)
        power = mem[b].power
        total = power[0]
        for k in range(1, 8):
            total = total + power[k]
        for part in range(2):
            mem[b].probes[0, 2, held[part], :] = total[part]

    def send_edges():
        plus, minus, out, rows = com.edge_plus, com.edge_minus, com.edge_out, com.edge_rows
        columns = iota((16, N), 1)
        spot = pl.ds(pl.multiple_of(16 * m, 16), 16)
        for j in range(2):
            row, column = place(com.where_own, 0, j)
            ahead = jnp.broadcast_to(row, (16, N)) >= 0
            first = columns >= column
            for part in range(2):
                low = jnp.where(ahead, plus[part, :, :N], minus[part, :, :N])
                high = jnp.where(ahead, plus[part, :, N:], minus[part, :, N:])
                out[j, part] = jnp.where(first, low, high)
        copies = [
            send(out.at[k % 2], rows.at[:, spot], t, lax.rem(m + k, 8)) for k in range(1, 8)
        ]
        rows[:, spot] = out[0]
        return copies

    def join_edges():
        rows, patch = com.edge_rows, mem[0].patch
        row, column = place(com.where_own, 0, 0)
        columns = iota((HALF, N), 1)
        first = columns >= column
        for half in range(2):
            span = slice(HALF * half, HALF * (half + 1))
            ahead = HALF * half + iota((HALF, N), 0) - row
            inside = (ahead >= 0) & (ahead < N)
            for part in range(2):
                own = jnp.where(first, obj[part, span, :N], obj[part, span, N:])
                patch[part, span, :] = jnp.where(inside, own, rows[part])

    def send_patches(b, field, halo):
        out, patch = mem[b].pout, mem[b].patch
        rows = own_row + iota((OWN, N), 0)
        columns = iota((OWN, N), 1)
        for j in range(2):
            row, column = place(com.where_own, b, j)
            ahead = rows - row
            inside = (ahead >= 0) & (ahead < N)
            first = columns >= column
            for part in range(2):
                low = jnp.where(inside, field[part, :, :N], halo[part, :, :N])
                high = jnp.where(inside, field[part, :, N:], halo[part, :, N:])
                out[j, part] = jnp.where(first, low, high)
        copies = []
        for k in range(1, 8):
            copies.append(
                send(out.at[k % 2], patch.at[:, pl.ds(own_row, OWN)], t, lax.rem(m + k, 8))
            )
        patch[:, pl.ds(own_row, OWN)] = out[0]
        return copies

    def shifted(real, imag, row, column):
        i0, i1 = iota((N, N), 0), iota((N, N), 1)
        pick = (((i0 + row) & (N - 1)) == i1).astype(F32).astype(BF16)
        both = real if imag is None else jnp.concatenate([real, imag], axis=1)
        high, low = halves(both)
        moved = dot(jnp.concatenate([pick, pick], axis=1), jnp.concatenate([high, low], axis=0))
        pick = (((i1 + column) & (N - 1)) == i0).astype(F32).astype(BF16)
        if imag is not None:
            moved = jnp.concatenate([moved[:, :N], moved[:, N:]], axis=0)
        high, low = halves(moved)
        moved = dot(jnp.concatenate([high, low], axis=1), jnp.concatenate([pick, pick], axis=0))
        return moved[:N], moved[N:]

    def roll_probes(b):
        row, column = place(com.where_own, b, 0)
        probes = mem[b].probes
        for mode in range(2):
            rolled[mode, 0], rolled[mode, 1] = shifted(
                probes[mode, 0], probes[mode, 1], -row, -column
            )

    def unroll_step(b, mode):
        row, column = place(com.where_own, b, 0)
        dstep = mem[b].dstep
        dstep[mode, 0], dstep[mode, 1] = shifted(dstep[mode, 0], dstep[mode, 1], row, column)

    def unrolled_one(field, b):
        row, column = place(com.where_own, b, 0)
        return shifted(field, None, row, column)[0]

    def chunk_rows(q):
        return pl.ds(pl.multiple_of(q * 64, 64), 64)

    stage = com.stage

    def right_stage(mode, q, real, imag, sign):
        high, low = halves(jnp.concatenate([real, imag], axis=0))
        product = dot(jnp.concatenate([high, high, low], axis=1), rw[...])
        out_real = product[:64, :N] + sign * product[64:, N:]
        out_imag = product[64:, :N] - sign * product[:64, N:]
        high, low = halves(jnp.concatenate([out_real, out_imag], axis=1))
        stage[mode, pl.ds(pl.multiple_of(q * 64, 64), 64), :] = high
        stage[mode, pl.ds(pl.multiple_of(N + q * 64, 64), 64), :] = low
        stage[mode, pl.ds(pl.multiple_of(2 * N + q * 64, 64), 64), :] = high

    def left_stage(mode, q, sign):
        product = dot(lw[q], stage[mode])
        return (
            product[:64, :N] + sign * product[64:, N:],
            product[:64, N:] - sign * product[64:, :N],
        )

    far, rolled = com.far, com.rolled

    def forward(b):
        ofield, inten = mem[b].patch, mem[b].inten

        def first(q, carry):
            rows = chunk_rows(q)
            o_real, o_imag = ofield[0, rows, :], ofield[1, rows, :]
            for mode in range(2):
                p_real, p_imag = rolled[mode, 0, rows, :], rolled[mode, 1, rows, :]
                right_stage(
                    mode,
                    q,
                    p_real * o_real - p_imag * o_imag,
                    p_real * o_imag + p_imag * o_real,
                    1.0,
                )
            return carry

        lax.fori_loop(0, 4, first, 0)

        irecv, copies = mem[b].irecv, []
        for k in (1, 2, 3, 0):
            q = lax.rem(z + k, 4)
            rows = chunk_rows(q)
            total = None
            for mode in range(2):
                f_real, f_imag = left_stage(mode, q, 1.0)
                far[mode, 0, rows, :] = f_real
                far[mode, 1, rows, :] = f_imag
                power = f_real * f_real + f_imag * f_imag
                total = power if total is None else total + power
            inten[rows, :] = total
            if k:
                copies.append(send(inten.at[rows], irecv.at[k - 1], t, 2 * q + c))
        return copies

    def inverse(b, copies, between):
        ofield, factor = mem[b].patch, mem[b].factor
        grad, dstep, grecv = mem[b].grad, mem[b].dstep, mem[b].grecv

        for k in range(4):
            if k:
                arrived(copies[k - 1 : k])
            q = lax.rem(z - k + 4, 4)
            rows = chunk_rows(q)
            scale = factor[rows, :]
            for mode in range(2):
                right_stage(mode, q, scale * far[mode, 0, rows, :], scale * far[mode, 1, rows, :], -1.0)
        between()

        sends = [None] * 8
        for k in (2, 1, 3, 0):
            q = lax.rem(z + k, 4)
            rows = chunk_rows(q)
            o_real, o_imag = ofield[0, rows, :], ofield[1, rows, :]
            g_real = jnp.zeros((64, N), F32)
            g_imag = jnp.zeros((64, N), F32)
            for mode in range(2):
                c_real, c_imag = left_stage(mode, q, -1.0)
                p_real, p_imag = rolled[mode, 0, rows, :], rolled[mode, 1, rows, :]
                g_real = g_real + p_real * c_real + p_imag * c_imag
                g_imag = g_imag + p_real * c_imag - p_imag * c_real
                dstep[mode, 0, rows, :] = o_real * c_real + o_imag * c_imag
                dstep[mode, 1, rows, :] = o_real * c_imag - o_imag * c_real
            grad[0, rows, :] = g_real
            grad[1, rows, :] = g_imag
            for twin in range(2):
                if k == 0 and twin == 0:
                    continue
                core = c if twin == 0 else 1 - c
                part = pl.ds(pl.multiple_of(OWN * (2 * q + core), OWN), OWN)
                slot = 2 * k + twin
                sends[slot] = send(grad.at[:, part], grecv.at[slot - 1], t, 2 * q + core)
        return sends[1:]

    def masks(ref, b, j):
        rows = own_row + iota((OWN, N), 0)
        row, column = place(ref, b, j)
        ahead = rows - row
        inside = (ahead >= 0) & (ahead < N)
        first = iota((OWN, N), 1) >= column
        return inside, first

    def sides(ref, b, j, here):
        inside, first = masks(ref, b, j)
        if not here:
            inside = jnp.logical_not(inside)
        return inside & first, inside & jnp.logical_not(first)

    def illumination(b, with_halo):
        high, low = halves(mem[b].probes[0, 2])
        power = jnp.concatenate([high, low], axis=0)
        rows = own_row + iota((OWN, N), 0)
        lanes = iota((OWN, N), 1)
        refs = [com.where_own, com.where_minus] + ([com.where_plus] if with_halo else [])
        spots_of = [(ref, j) for ref in refs for j in range(2)]
        picks = []
        for ref, j in spots_of:
            row, _ = place(ref, b, j)
            pick = (((rows - row) & (N - 1)) == lanes).astype(F32).astype(BF16)
            picks.append(jnp.concatenate([pick, pick], axis=1))
        taken = dot(jnp.concatenate(picks, axis=0), power)
        i0, i1 = iota((N, N), 0), iota((N, N), 1)
        blocks = [[jnp.zeros((OWN, N), F32) for _ in range(2)] for _ in range(2)]
        for index, (ref, j) in enumerate(spots_of):
            _, column = place(ref, b, j)
            pick = (((i1 - column) & (N - 1)) == i0).astype(F32).astype(BF16)
            high, low = halves(taken[OWN * index : OWN * (index + 1)])
            moved = dot(
                jnp.concatenate([high, low], axis=1), jnp.concatenate([pick, pick], axis=0)
            )
            kind = index // 2
            for block, here in ((0, kind == 0), (1, kind == 2)):
                if (block, kind) in ((0, 2), (1, 1)):
                    continue
                for side_index, mask in enumerate(sides(ref, b, j, here)):
                    blocks[block][side_index] = blocks[block][side_index] + jnp.where(
                        mask, moved, 0.0
                    )
        for block in range(2 if with_halo else 1):
            com.illum[block, :, :N] = blocks[block][0]
            com.illum[block, :, N:] = blocks[block][1]

    def update_block(b, field, field_rows, new, block, steps):
        for part in range(2):
            for side_index, columns in ((0, slice(0, N)), (1, slice(N, WIDTH))):
                total = jnp.zeros((OWN, N), F32)
                for step, j, ref, here in steps:
                    total = total + jnp.where(sides(ref, b, j, here)[side_index], step[j, part], 0.0)
                new[part, :, columns] = field[part, field_rows, columns] + total / (
                    com.illum[block, :, columns] + 1.0
                )

    def refine():
        spot = pl.ds(pl.multiple_of(16 * m, 16), 16)
        far_spot = pl.ds(pl.multiple_of(HALF + 16 * m, 16), 16)
        edge_copies = [
            send(obj.at[:, spot], com.edge_plus, lax.rem(t + 31, 32), m),
            send(obj.at[:, far_spot], com.edge_minus, lax.rem(t + 1, 32), m),
        ]
        probe_copy = send(
            mem[0].probes.at[0, pl.ds(0, 2)], mem[0].probes.at[1, pl.ds(0, 2)], t, sibling
        )
        where_copies = [
            send(com.where_own, com.where_minus, t_plus, m),
            send(com.where_own, com.where_plus, t_minus, m),
        ]
        halo_copy = send(obj.at[:, pl.ds(own_row, OWN)], mem[0].halo, t_minus, m)
        arrived(edge_copies)
        patch_copies = send_edges()
        arrived([probe_copy])
        roll_probes(0)
        power_copies = send_power(
            0, [(probe[0, 0, held[part]], probe[0, 1, held[part]]) for part in range(2)]
        )
        arrived(where_copies)
        for load in loads:
            load.wait()
        for b in range(BATCHES):
            last = b == BATCHES - 1
            if b == 0:
                field, field_rows = obj, pl.ds(own_row, OWN)
            else:
                field, field_rows = mem[b - 1].objnew, slice(0, OWN)
            arrived(patch_copies)
            if b == 0:
                join_edges()
            if b:
                arrived([probe_copy])
                roll_probes(b)
            copies = forward(b)
            sum_power(b, power_copies)
            power_gather = Gather(lambda rows: mem[b].probes.at[0, 2, rows])
            power_gather.start_one()
            patch, cover = mem[b].patch, mem[b].cov
            cover[0] = unrolled_one(patch[0] * patch[0] + patch[1] * patch[1], b)
            cover_copy = send(cover, mem[b].csib, t, sibling)
            arrived([cover_copy])
            mem[b].cover_sum.full[...] = cover[...] + mem[b].csib[...]
            cover_sum = Reduce(mem[b].cover_sum)
            cover_sum.start_one()
            inten, irecv, factor = mem[b].inten, mem[b].irecv, mem[b].factor
            arrived(copies)
            own_rows = pl.ds(i_row, 64)
            total = inten[own_rows, :] + irecv[0] + irecv[1] + irecv[2]
            factor[own_rows, :] = (
                jnp.sqrt((observed[b, own_rows, :] + 1.0) / (total + 1.0)) - 1.0
            )
            copies = []
            for k in range(1, 4):
                other = lax.rem(z + k, 4)
                copies.append(send(factor.at[own_rows], factor.at[own_rows], t, 2 * other + c))
            power_gather.start_two()
            cover_sum.start_two()
            copies = inverse(b, copies, cover_sum.start_pair)
            grad, grecv, dstep = mem[b].grad, mem[b].grecv, mem[b].dstep
            unroll_step(b, 1)
            step_copy = send(dstep.at[1], mem[b].dsib, t, sibling)
            unroll_step(b, 0)
            power_gather.finish()
            arrived([step_copy])
            mem[b].probe_sum.full[...] = dstep[0] + mem[b].dsib[...]
            probe_sum = Reduce(mem[b].probe_sum)
            probe_sum.start_one()
            illumination(b, not last)
            probe_sum.start_two()
            arrived(copies)
            own, minus, plus = mem[b].gown, mem[b].gminus, mem[b].gplus
            own[0] = grad[:, pl.ds(own_row, OWN)] + grecv[1] + grecv[3] + grecv[5]
            own[1] = grecv[0] + grecv[2] + grecv[4] + grecv[6]
            copies = [send(own, minus, t_plus, m)]
            if not last:
                copies.append(send(own, plus, t_minus, m))
            probe_sum.start_pair()
            if b == 0:
                arrived([halo_copy])
            arrived(copies)
            own_steps = [(own, j, com.where_own, True) for j in range(2)]
            own_steps += [(minus, j, com.where_minus, False) for j in range(2)]
            new = mem[b].objnew
            update_block(b, field, field_rows, new, 0, own_steps)
            if last:
                rows = pl.ds(own_row, OWN)
                final_copies = []
                for k in range(1, 4):
                    other = 2 * lax.rem(z + k, 4) + c
                    final_copies.append(send(new, out_obj.at[:, rows], t, other))
                sibling_copies = [send(new, out_obj.at[:, rows], t, sibling)]
                out_obj[:, rows] = new[...]
            else:
                halo_steps = [(plus, j, com.where_plus, True) for j in range(2)]
                halo_steps += [(own, j, com.where_own, False) for j in range(2)]
                halo = mem[b + 1].halo
                update_block(b, mem[b].halo, slice(0, OWN), halo, 1, halo_steps)
                patch_copies = send_patches(b + 1, new, halo)
            coverage = cover_sum.finish()
            step = probe_sum.finish()
            probes = mem[b].probes
            following = out_probe if last else mem[b + 1].probes
            values = []
            for half in range(2):
                values.append(
                    [
                        probes[0, part, held[half], :]
                        + step[half][part] / (coverage[half][0] + 1.0)
                        for part in range(2)
                    ]
                )
                for part in range(2):
                    following[0, part, held[half], :] = values[half][part]
            gather = Gather(lambda rows: following.at[0, pl.ds(0, 2), rows])
            gather.start_one()
            gather.start_two()
            if last:
                for k in range(1, 4):
                    arrived(final_copies[k - 1 : k])
                    other = 2 * lax.rem(z - k + 4, 4) + c
                    rows = pl.ds(pl.multiple_of(OWN * other, OWN), OWN)
                    part = out_obj.at[:, rows]
                    sibling_copies.append(send(part, part, t, sibling))
                gather.finish()
                arrived(sibling_copies)
            else:
                power_copies = send_power(b + 1, values)
                gather.finish()
                probe_copy = send(
                    following.at[0, pl.ds(0, 2)], following.at[1, pl.ds(0, 2)], t, sibling
                )

    refine()
    for copy in sent:
        copy.wait_send()


def shards(object_field, probe, positions, measured):
    right, left = split_tables()
    plan = scratch_plan()
    leaves, tree = jax.tree.flatten(plan)

    def body(*refs):
        kernel(tree, *refs)

    vmem = pl.BlockSpec(memory_space=pltpu.VMEM)
    anywhere = pl.BlockSpec(memory_space=pl.ANY)
    return pl.pallas_call(
        body,
        name="refine",
        out_shape=(
            jax.ShapeDtypeStruct(object_field.shape, F32),
            jax.ShapeDtypeStruct(probe.shape, F32),
        ),
        in_specs=[pl.BlockSpec(memory_space=pltpu.SMEM)] + [vmem] * 2 + [anywhere] * 3,
        out_specs=(vmem, vmem),
        scratch_shapes=leaves
        + [pltpu.SemaphoreType.DMA((count,)) for count in (COPIES, COPIES, 4)],
        compiler_params=pltpu.CompilerParams(
            collective_id=0, has_side_effects=True, vmem_limit_bytes=30 * 1024 * 1024
        ),
    )(positions, object_field, probe, measured, jnp.asarray(right), jnp.asarray(left))


def solution(mesh):
    in_specs = (
        P(None, "tile", None),
        P("mode", None, None, None),
        P(None, "tile", None),
        P(None, "tile", None, None),
    )
    out_specs = (P(None, "tile", None), P("mode", None, None, None))
    return jax.shard_map(shards, mesh=mesh, in_specs=in_specs, out_specs=out_specs, check_vma=False)
```

time: 191 us -> 145 us (0.76)
  the two profiles are of different devices: /device:TPU:1 before, /device:TPU:97 now
where the time goes in v2:
time: 145 us
  Pallas kernels  136 us (94%)
  local copies, waits for them, and re-layouts  8.19 us (6%)
    pallas_call x1, Pallas kernels, shards(): pl.pallas_call(body, name='refine', out_shape=(jax.ShapeDtypeStruct(objec...  136 us
    unnamed x14, local copies, waits for them, and re-layouts  8.19 us

profile of v2, /device:TPU:97, one launch (start us, length us, event | category | flops | bytes accessed | tf_op | source)
XLA Modules:
  0.0 145.0 jit_solution(40966805402278139)
XLA Ops:
  0.6 0.0 copy-start
  0.6 1.2 copy-done
  1.9 0.0 copy-start.1
  1.9 1.2 copy-done.1
  3.1 0.0 copy-start.2
  3.1 1.1 copy-done.2
  4.2 0.0 copy-start.3
  4.2 1.1 copy-done.3
  5.3 0.0 copy-start.4
  5.4 1.0 copy-done.4
  6.4 0.0 copy-start.5
  6.4 0.7 copy-done.5
  7.1 136.2 %refine.1 = (f32[2,256,512]{2,1,0:T(8,128)S(1)}, f32[1,2,256,256]{3,2,1,0:T(8,128)S(1)}) custom-call(s32[2,2,2]{2,1,0:T(2,128)S(1)} %copy-done.5, f32[2,256,512]{2,1,0:T(8,128)S(1)} %copy-done, f32[1,2,256,256]{3,2,1,0:T(8,128)S(1)} %copy-done.4, f32[2,2,256,256]{3,2,1,0:T(8,128)S(1)} %copy-done.1, bf16[768,512]{1,0:T(8,128)(2,1)S(1)} %copy-done.3, ...), custom_call_target="tpu_custom_call" | custom-call | tf_op jit(solution)/shard_map/refine/pallas_call | solution.py:689
  143.3 1.0 copy.10
  144.2 0.8 copy.11
Async XLA Ops:
  0.6 1.2 copy-start
  1.9 1.2 copy-start.1
  3.1 1.1 copy-start.2
  4.2 1.1 copy-start.3
  5.3 1.0 copy-start.4
  6.4 0.7 copy-start.5

commit v3 on v2

--- a/solution.py
+++ b/solution.py
@@ -119,7 +119,7 @@
             setattr(self, name, Box(entry) if isinstance(entry, dict) else entry)
 
 
-COPIES = 200
+COPIES = 248
 
 
 def kernel(tree, pos, obj, probe, measured, rtable, ltable, out_obj, out_probe, *scratch):
@@ -328,7 +328,7 @@
                 own = jnp.where(first, obj[part, span, :N], obj[part, span, N:])
                 patch[part, span, :] = jnp.where(inside, own, rows[part])
 
-    def send_patches(b, field, halo):
+    def send_patches(b, field, halo, part):
         out, patch = mem[b].pout, mem[b].patch
         rows = own_row + iota((OWN, N), 0)
         columns = iota((OWN, N), 1)
@@ -337,16 +337,14 @@
             ahead = rows - row
             inside = (ahead >= 0) & (ahead < N)
             first = columns >= column
-            for part in range(2):
-                low = jnp.where(inside, field[part, :, :N], halo[part, :, :N])
-                high = jnp.where(inside, field[part, :, N:], halo[part, :, N:])
-                out[j, part] = jnp.where(first, low, high)
+            low = jnp.where(inside, field[part, :, :N], halo[part, :, :N])
+            high = jnp.where(inside, field[part, :, N:], halo[part, :, N:])
+            out[j, part] = jnp.where(first, low, high)
         copies = []
+        spot = patch.at[part, pl.ds(own_row, OWN)]
         for k in range(1, 8):
-            copies.append(
-                send(out.at[k % 2], patch.at[:, pl.ds(own_row, OWN)], t, lax.rem(m + k, 8))
-            )
-        patch[:, pl.ds(own_row, OWN)] = out[0]
+            copies.append(send(out.at[k % 2, part], spot, t, lax.rem(m + k, 8)))
+        patch[part, pl.ds(own_row, OWN)] = out[0, part]
         return copies
 
     def shifted(real, imag, row, column):
@@ -452,7 +450,7 @@
                 right_stage(mode, q, scale * far[mode, 0, rows, :], scale * far[mode, 1, rows, :], -1.0)
         between()
 
-        sends = [None] * 8
+        sends, later = [], []
         for k in (2, 1, 3, 0):
             q = lax.rem(z + k, 4)
             rows = chunk_rows(q)
@@ -473,9 +471,10 @@
                     continue
                 core = c if twin == 0 else 1 - c
                 part = pl.ds(pl.multiple_of(OWN * (2 * q + core), OWN), OWN)
-                slot = 2 * k + twin
-                sends[slot] = send(grad.at[:, part], grecv.at[slot - 1], t, 2 * q + core)
-        return sends[1:]
+                slot = 2 * k + twin - 1
+                sends.append(send(grad.at[0, part], grecv.at[slot, 0], t, 2 * q + core))
+                later.append((grad.at[1, part], grecv.at[slot, 1], t, 2 * q + core))
+        return [sends, [send(*args) for args in later]]
 
     def masks(ref, b, j):
         rows = own_row + iota((OWN, N), 0)
@@ -525,15 +524,14 @@
             com.illum[block, :, :N] = blocks[block][0]
             com.illum[block, :, N:] = blocks[block][1]
 
-    def update_block(b, field, field_rows, new, block, steps):
-        for part in range(2):
-            for side_index, columns in ((0, slice(0, N)), (1, slice(N, WIDTH))):
-                total = jnp.zeros((OWN, N), F32)
-                for step, j, ref, here in steps:
-                    total = total + jnp.where(sides(ref, b, j, here)[side_index], step[j, part], 0.0)
-                new[part, :, columns] = field[part, field_rows, columns] + total / (
-                    com.illum[block, :, columns] + 1.0
-                )
+    def update_block(b, part, field, field_rows, new, block, steps):
+        for side_index, columns in ((0, slice(0, N)), (1, slice(N, WIDTH))):
+            total = jnp.zeros((OWN, N), F32)
+            for step, j, ref, here in steps:
+                total = total + jnp.where(sides(ref, b, j, here)[side_index], step[j, part], 0.0)
+            new[part, :, columns] = field[part, field_rows, columns] + total / (
+                com.illum[block, :, columns] + 1.0
+            )
 
     def refine():
         spot = pl.ds(pl.multiple_of(16 * m, 16), 16)
@@ -607,36 +605,47 @@
             probe_sum = Reduce(mem[b].probe_sum)
             probe_sum.start_one()
             illumination(b, not last)
-            probe_sum.start_two()
-            arrived(copies)
             own, minus, plus = mem[b].gown, mem[b].gminus, mem[b].gplus
-            own[0] = grad[:, pl.ds(own_row, OWN)] + grecv[1] + grecv[3] + grecv[5]
-            own[1] = grecv[0] + grecv[2] + grecv[4] + grecv[6]
-            copies = [send(own, minus, t_plus, m)]
-            if not last:
-                copies.append(send(own, plus, t_minus, m))
+            near = []
+            for part in range(2):
+                arrived(copies[part])
+                here = grad[part, pl.ds(own_row, OWN)]
+                own[0, part] = here + grecv[1, part] + grecv[3, part] + grecv[5, part]
+                own[1, part] = (
+                    grecv[0, part] + grecv[2, part] + grecv[4, part] + grecv[6, part]
+                )
+                near.append([send(own.at[:, part], minus.at[:, part], t_plus, m)])
+                if not last:
+                    near[part].append(send(own.at[:, part], plus.at[:, part], t_minus, m))
+                if part == 0:
+                    probe_sum.start_two()
             probe_sum.start_pair()
             if b == 0:
                 arrived([halo_copy])
-            arrived(copies)
             own_steps = [(own, j, com.where_own, True) for j in range(2)]
             own_steps += [(minus, j, com.where_minus, False) for j in range(2)]
+            halo_steps = [(plus, j, com.where_plus, True) for j in range(2)]
+            halo_steps += [(own, j, com.where_own, False) for j in range(2)]
             new = mem[b].objnew
-            update_block(b, field, field_rows, new, 0, own_steps)
-            if last:
-                rows = pl.ds(own_row, OWN)
-                final_copies = []
-                for k in range(1, 4):
-                    other = 2 * lax.rem(z + k, 4) + c
-                    final_copies.append(send(new, out_obj.at[:, rows], t, other))
-                sibling_copies = [send(new, out_obj.at[:, rows], t, sibling)]
-                out_obj[:, rows] = new[...]
-            else:
-                halo_steps = [(plus, j, com.where_plus, True) for j in range(2)]
-                halo_steps += [(own, j, com.where_own, False) for j in range(2)]
-                halo = mem[b + 1].halo
-                update_block(b, mem[b].halo, slice(0, OWN), halo, 1, halo_steps)
-                patch_copies = send_patches(b + 1, new, halo)
+            final_copies, sibling_copies, patch_copies = [], [], []
+            for part in range(2):
+                arrived(near[part])
+                update_block(b, part, field, field_rows, new, 0, own_steps)
+                if last:
+                    rows = pl.ds(own_row, OWN)
+                    spot = out_obj.at[part, rows]
+                    final_copies.append(
+                        [
+                            send(new.at[part], spot, t, 2 * lax.rem(z + k, 4) + c)
+                            for k in range(1, 4)
+                        ]
+                    )
+                    sibling_copies.append(send(new.at[part], spot, t, sibling))
+                    out_obj[part, rows] = new[part]
+                else:
+                    halo = mem[b + 1].halo
+                    update_block(b, part, mem[b].halo, slice(0, OWN), halo, 1, halo_steps)
+                    patch_copies += send_patches(b + 1, new, halo, part)
             coverage = cover_sum.finish()
             step = probe_sum.finish()
             probes = mem[b].probes
@@ -656,12 +665,13 @@
             gather.start_one()
             gather.start_two()
             if last:
-                for k in range(1, 4):
-                    arrived(final_copies[k - 1 : k])
-                    other = 2 * lax.rem(z - k + 4, 4) + c
-                    rows = pl.ds(pl.multiple_of(OWN * other, OWN), OWN)
-                    part = out_obj.at[:, rows]
-                    sibling_copies.append(send(part, part, t, sibling))
+                for part in range(2):
+                    for k in range(1, 4):
+                        arrived(final_copies[part][k - 1 : k])
+                        other = 2 * lax.rem(z - k + 4, 4) + c
+                        rows = pl.ds(pl.multiple_of(OWN * other, OWN), OWN)
+                        spot = out_obj.at[part, rows]
+                        sibling_copies.append(send(spot, spot, t, sibling))
                 gather.finish()
                 arrived(sibling_copies)
             else:

time: 145 us -> 142 us (0.979)
  the two profiles are of different devices: /device:TPU:97 before, /device:TPU:1 now
where the time goes in v3:
time: 142 us; the launch traced here: 141 us
  Pallas kernels  132 us (93%)
  local copies, waits for them, and re-layouts  8.19 us (6%)
    pallas_call x1, Pallas kernels, shards(): pl.pallas_call(body, name='refine', out_shape=(jax.ShapeDtypeStruct(objec...  132 us
    unnamed x14, local copies, waits for them, and re-layouts  8.19 us

profile of v3, /device:TPU:1, one launch (start us, length us, event | category | flops | bytes accessed | tf_op | source)
XLA Modules:
  0.0 140.6 jit_solution(2630497298982017711)
XLA Ops:
  0.6 0.0 copy-start
  0.6 1.2 copy-done
  1.9 0.0 copy-start.1
  1.9 1.2 copy-done.1
  3.1 0.0 copy-start.2
  3.1 1.1 copy-done.2
  4.2 0.0 copy-start.3
  4.2 1.1 copy-done.3
  5.3 0.0 copy-start.4
  5.4 1.0 copy-done.4
  6.4 0.0 copy-start.5
  6.4 0.7 copy-done.5
  7.1 131.8 %refine.1 = (f32[2,256,512]{2,1,0:T(8,128)S(1)}, f32[1,2,256,256]{3,2,1,0:T(8,128)S(1)}) custom-call(s32[2,2,2]{2,1,0:T(2,128)S(1)} %copy-done.5, f32[2,256,512]{2,1,0:T(8,128)S(1)} %copy-done, f32[1,2,256,256]{3,2,1,0:T(8,128)S(1)} %copy-done.4, f32[2,2,256,256]{3,2,1,0:T(8,128)S(1)} %copy-done.1, bf16[768,512]{1,0:T(8,128)(2,1)S(1)} %copy-done.3, ...), custom_call_target="tpu_custom_call" | custom-call | tf_op jit(solution)/shard_map/refine/pallas_call | solution.py:699
  138.9 1.0 copy.10
  139.8 0.8 copy.11
Async XLA Ops:
  0.6 1.2 copy-start
  1.9 1.2 copy-start.1
  3.1 1.1 copy-start.2
  4.2 1.1 copy-start.3
  5.3 1.0 copy-start.4
  6.4 0.7 copy-start.5

commit v4 on v3

--- a/solution.py
+++ b/solution.py
@@ -120,11 +120,12 @@
 
 
 COPIES = 248
+RELAYS = 12
 
 
 def kernel(tree, pos, obj, probe, measured, rtable, ltable, out_obj, out_probe, *scratch):
-    ssem, rsem, lsem = scratch[-3:]
-    com, *mem = [Box(entries) for entries in jax.tree.unflatten(tree, scratch[:-3])]
+    ssem, rsem, lsem, slots, relay_sem = scratch[-5:]
+    com, *mem = [Box(entries) for entries in jax.tree.unflatten(tree, scratch[:-5])]
     t = lax.axis_index("tile")
     m = lax.axis_index("mode")
     x, zh, y = t // 8, (t // 4) % 2, t % 4
@@ -138,13 +139,13 @@
     i_row = pl.multiple_of(64 * z, 64)
     sent = []
 
-    def send(src, dst, tile, mode):
+    def send(src, dst, tile, mode, slot=None):
         index = len(sent)
         copy = pltpu.make_async_remote_copy(
             src_ref=src,
             dst_ref=dst,
             send_sem=ssem.at[index],
-            recv_sem=rsem.at[index],
+            recv_sem=rsem.at[index] if slot is None else slots.at[slot],
             device_id=(tile, mode),
             device_id_type=MESH,
         )
@@ -155,6 +156,30 @@
     def arrived(copies):
         for copy in copies:
             copy.wait_recv()
+
+    mate = z + 1 - 2 * (z % 2)
+    cross = 2 - z // 2
+    cross_mate = cross + 1 - 2 * (cross % 2)
+    inner = (z == 1) | (z == 2)
+    outer_class = jnp.where(inner, 0, 1)
+    relayed = []
+
+    def relay(slot, part):
+        copy = pltpu.make_async_remote_copy(
+            src_ref=part,
+            dst_ref=part,
+            send_sem=relay_sem.at[slot],
+            recv_sem=slots.at[slot],
+            device_id=(t, 2 * mate + c),
+            device_id_type=MESH,
+        )
+        copy.wait_recv()
+
+        @pl.when(inner)
+        def _():
+            copy.start()
+
+        relayed.append(copy)
 
     def y_tile(k):
         other = lax.rem(y + k, 4)
@@ -328,6 +353,23 @@
                 own = jnp.where(first, obj[part, span, :N], obj[part, span, N:])
                 patch[part, span, :] = jnp.where(inside, own, rows[part])
 
+    def relay_patches(b, part):
+        for place_class, chip in enumerate((cross, cross_mate)):
+            for twin in range(2):
+                core = c if twin == 0 else 1 - c
+                rows = pl.ds(pl.multiple_of(OWN * (2 * chip + core), OWN), OWN)
+                relay(4 * part + 2 * place_class + twin, mem[b].patch.at[part, rows])
+
+    def relay_final(part, final_copies, sibling_copies):
+        for index, chip in enumerate((mate, cross, cross_mate)):
+            rows = pl.ds(pl.multiple_of(OWN * (2 * chip + c), OWN), OWN)
+            spot = out_obj.at[part, rows]
+            if index:
+                relay(8 + 2 * part + index - 1, spot)
+            else:
+                arrived(final_copies[part : part + 1])
+            sibling_copies.append(send(spot, spot, t, sibling))
+
     def send_patches(b, field, halo, part):
         out, patch = mem[b].pout, mem[b].patch
         rows = own_row + iota((OWN, N), 0)
@@ -342,8 +384,14 @@
             out[j, part] = jnp.where(first, low, high)
         copies = []
         spot = patch.at[part, pl.ds(own_row, OWN)]
-        for k in range(1, 8):
-            copies.append(send(out.at[k % 2, part], spot, t, lax.rem(m + k, 8)))
+        for twin in range(2):
+            core = c if twin == 0 else 1 - c
+            slot = 4 * part + 2 * outer_class + twin
+            send(out.at[twin, part], spot, t, 2 * cross + core, slot)
+        for twin in range(2):
+            core = c if twin == 0 else 1 - c
+            copies.append(send(out.at[twin, part], spot, t, 2 * mate + core))
+        copies.append(send(out.at[1, part], spot, t, sibling))
         patch[part, pl.ds(own_row, OWN)] = out[0, part]
         return copies
 
@@ -634,18 +682,19 @@
                 if last:
                     rows = pl.ds(own_row, OWN)
                     spot = out_obj.at[part, rows]
-                    final_copies.append(
-                        [
-                            send(new.at[part], spot, t, 2 * lax.rem(z + k, 4) + c)
-                            for k in range(1, 4)
-                        ]
-                    )
+                    slot = 8 + 2 * part + outer_class
+                    send(new.at[part], spot, t, 2 * cross + c, slot)
+                    final_copies.append(send(new.at[part], spot, t, 2 * mate + c))
                     sibling_copies.append(send(new.at[part], spot, t, sibling))
                     out_obj[part, rows] = new[part]
                 else:
                     halo = mem[b + 1].halo
                     update_block(b, part, mem[b].halo, slice(0, OWN), halo, 1, halo_steps)
                     patch_copies += send_patches(b + 1, new, halo, part)
+            if last:
+                relay_final(0, final_copies, sibling_copies)
+            else:
+                relay_patches(b + 1, 0)
             coverage = cover_sum.finish()
             step = probe_sum.finish()
             probes = mem[b].probes
@@ -663,15 +712,12 @@
                     following[0, part, held[half], :] = values[half][part]
             gather = Gather(lambda rows: following.at[0, pl.ds(0, 2), rows])
             gather.start_one()
+            if last:
+                relay_final(1, final_copies, sibling_copies)
+            else:
+                relay_patches(b + 1, 1)
             gather.start_two()
             if last:
-                for part in range(2):
-                    for k in range(1, 4):
-                        arrived(final_copies[part][k - 1 : k])
-                        other = 2 * lax.rem(z - k + 4, 4) + c
-                        rows = pl.ds(pl.multiple_of(OWN * other, OWN), OWN)
-                        spot = out_obj.at[part, rows]
-                        sibling_copies.append(send(spot, spot, t, sibling))
                 gather.finish()
                 arrived(sibling_copies)
             else:
@@ -682,6 +728,8 @@
                 )
 
     refine()
+    for copy in relayed:
+        pl.when(inner)(copy.wait_send)
     for copy in sent:
         copy.wait_send()
 
@@ -706,7 +754,7 @@
         in_specs=[pl.BlockSpec(memory_space=pltpu.SMEM)] + [vmem] * 2 + [anywhere] * 3,
         out_specs=(vmem, vmem),
         scratch_shapes=leaves
-        + [pltpu.SemaphoreType.DMA((count,)) for count in (COPIES, COPIES, 4)],
+        + [pltpu.SemaphoreType.DMA((count,)) for count in (COPIES, COPIES, 4, RELAYS, RELAYS)],
         compiler_params=pltpu.CompilerParams(
             collective_id=0, has_side_effects=True, vmem_limit_bytes=30 * 1024 * 1024
         ),

time: 142 us -> 159 us (1.12)
  Pallas kernels: 132 us -> 149 us
    pallas_call x1, Pallas kernels: 132 us -> 149 us  [shards(): pl.pallas_call(body, name='refine', out_shape=(jax.ShapeDtypeStruct(objec...]
where the time goes in v4:
time: 159 us; the launch traced here: 158 us
  Pallas kernels  149 us (94%)
  local copies, waits for them, and re-layouts  8.19 us (5%)
    pallas_call x1, Pallas kernels, shards(): pl.pallas_call(body, name='refine', out_shape=(jax.ShapeDtypeStruct(objec...  149 us
    unnamed x14, local copies, waits for them, and re-layouts  8.19 us

profile of v4, /device:TPU:1, one launch (start us, length us, event | category | flops | bytes accessed | tf_op | source)
XLA Modules:
  0.0 157.8 jit_solution(1287768218315418637)
XLA Ops:
  0.6 0.0 copy-start
  0.6 1.2 copy-done
  1.9 0.0 copy-start.1
  1.9 1.2 copy-done.1
  3.1 0.0 copy-start.2
  3.1 1.1 copy-done.2
  4.2 0.0 copy-start.3
  4.2 1.1 copy-done.3
  5.3 0.0 copy-start.4
  5.4 1.0 copy-done.4
  6.4 0.0 copy-start.5
  6.4 0.7 copy-done.5
  7.1 149.0 %refine.1 = (f32[2,256,512]{2,1,0:T(8,128)S(1)}, f32[1,2,256,256]{3,2,1,0:T(8,128)S(1)}) custom-call(s32[2,2,2]{2,1,0:T(2,128)S(1)} %copy-done.5, f32[2,256,512]{2,1,0:T(8,128)S(1)} %copy-done, f32[1,2,256,256]{3,2,1,0:T(8,128)S(1)} %copy-done.4, f32[2,2,256,256]{3,2,1,0:T(8,128)S(1)} %copy-done.1, bf16[768,512]{1,0:T(8,128)(2,1)S(1)} %copy-done.3, ...), custom_call_target="tpu_custom_call" | custom-call | tf_op jit(solution)/shard_map/refine/pallas_call | solution.py:747
  156.0 1.0 copy.10
  157.0 0.8 copy.11
Async XLA Ops:
  0.6 1.2 copy-start
  1.9 1.2 copy-start.1
  3.1 1.1 copy-start.2
  4.2 1.1 copy-start.3
  5.3 1.0 copy-start.4
  6.4 0.7 copy-start.5

commit v5 on v3

--- a/solution.py
+++ b/solution.py
@@ -130,11 +130,20 @@
     x, zh, y = t // 8, (t // 4) % 2, t % 4
     z, c = m // 2, m % 2
     sibling = m + 1 - 2 * c
-    side = 1 - 2 * (m // 4)
+
+    def mirrored(chip):
+        return chip + zh * (3 - 2 * chip)
+
+    def facing(tile):
+        flip = jnp.abs((tile // 4) % 2 - zh)
+        return 2 * (z + flip * (3 - 2 * z)) + c
+
+    block = 2 * mirrored(z) + c
+    side = 1 - 2 * (block // 4)
     t_plus = lax.rem(t + side + 32, 32)
     t_minus = lax.rem(t - side + 32, 32)
     t_pair = t + 4 - 8 * zh
-    own_row = pl.multiple_of(OWN * m, OWN)
+    own_row = pl.multiple_of(OWN * block, OWN)
     i_row = pl.multiple_of(64 * z, 64)
     sent = []
 
@@ -175,7 +184,7 @@
     partners = [(t, lax.rem(m + k, 8)) for k in range(1, 8)]
     partners += [(y_tile(k)[1], m) for k in range(1, 4)]
     partners += [(x_tile(k)[1], m) for k in range(1, 4)]
-    partners += [(t_pair, m), (t_plus, m), (t_minus, m)]
+    partners += [(t_pair, m), (t_plus, facing(t_plus)), (t_minus, facing(t_minus))]
     for partner in partners:
         pl.semaphore_signal(barrier, inc=1, device_id=partner, device_id_type=MESH)
     for load in loads:
@@ -300,7 +309,7 @@
     def send_edges():
         plus, minus, out, rows = com.edge_plus, com.edge_minus, com.edge_out, com.edge_rows
         columns = iota((16, N), 1)
-        spot = pl.ds(pl.multiple_of(16 * m, 16), 16)
+        spot = pl.ds(pl.multiple_of(16 * block, 16), 16)
         for j in range(2):
             row, column = place(com.where_own, 0, j)
             ahead = jnp.broadcast_to(row, (16, N)) >= 0
@@ -453,12 +462,13 @@
         sends, later = [], []
         for k in (2, 1, 3, 0):
             q = lax.rem(z + k, 4)
-            rows = chunk_rows(q)
+            chunk = mirrored(q)
+            rows = chunk_rows(chunk)
             o_real, o_imag = ofield[0, rows, :], ofield[1, rows, :]
             g_real = jnp.zeros((64, N), F32)
             g_imag = jnp.zeros((64, N), F32)
             for mode in range(2):
-                c_real, c_imag = left_stage(mode, q, -1.0)
+                c_real, c_imag = left_stage(mode, chunk, -1.0)
                 p_real, p_imag = rolled[mode, 0, rows, :], rolled[mode, 1, rows, :]
                 g_real = g_real + p_real * c_real + p_imag * c_imag
                 g_imag = g_imag + p_real * c_imag - p_imag * c_real
@@ -470,7 +480,7 @@
                 if k == 0 and twin == 0:
                     continue
                 core = c if twin == 0 else 1 - c
-                part = pl.ds(pl.multiple_of(OWN * (2 * q + core), OWN), OWN)
+                part = pl.ds(pl.multiple_of(OWN * (2 * chunk + core), OWN), OWN)
                 slot = 2 * k + twin - 1
                 sends.append(send(grad.at[0, part], grecv.at[slot, 0], t, 2 * q + core))
                 later.append((grad.at[1, part], grecv.at[slot, 1], t, 2 * q + core))
@@ -534,20 +544,21 @@
             )
 
     def refine():
-        spot = pl.ds(pl.multiple_of(16 * m, 16), 16)
-        far_spot = pl.ds(pl.multiple_of(HALF + 16 * m, 16), 16)
+        spot = pl.ds(pl.multiple_of(16 * block, 16), 16)
+        far_spot = pl.ds(pl.multiple_of(HALF + 16 * block, 16), 16)
+        below, above = lax.rem(t + 31, 32), lax.rem(t + 1, 32)
         edge_copies = [
-            send(obj.at[:, spot], com.edge_plus, lax.rem(t + 31, 32), m),
-            send(obj.at[:, far_spot], com.edge_minus, lax.rem(t + 1, 32), m),
+            send(obj.at[:, spot], com.edge_plus, below, facing(below)),
+            send(obj.at[:, far_spot], com.edge_minus, above, facing(above)),
         ]
         probe_copy = send(
             mem[0].probes.at[0, pl.ds(0, 2)], mem[0].probes.at[1, pl.ds(0, 2)], t, sibling
         )
         where_copies = [
-            send(com.where_own, com.where_minus, t_plus, m),
-            send(com.where_own, com.where_plus, t_minus, m),
+            send(com.where_own, com.where_minus, t_plus, facing(t_plus)),
+            send(com.where_own, com.where_plus, t_minus, facing(t_minus)),
         ]
-        halo_copy = send(obj.at[:, pl.ds(own_row, OWN)], mem[0].halo, t_minus, m)
+        halo_copy = send(obj.at[:, pl.ds(own_row, OWN)], mem[0].halo, t_minus, facing(t_minus))
         arrived(edge_copies)
         patch_copies = send_edges()
         arrived([probe_copy])
@@ -614,9 +625,9 @@
                 own[1, part] = (
                     grecv[0, part] + grecv[2, part] + grecv[4, part] + grecv[6, part]
                 )
-                near.append([send(own.at[:, part], minus.at[:, part], t_plus, m)])
+                near.append([send(own.at[:, part], minus.at[:, part], t_plus, facing(t_plus))])
                 if not last:
-                    near[part].append(send(own.at[:, part], plus.at[:, part], t_minus, m))
+                    near[part].append(send(own.at[:, part], plus.at[:, part], t_minus, facing(t_minus)))
                 if part == 0:
                     probe_sum.start_two()
             probe_sum.start_pair()
@@ -668,7 +679,7 @@
                 for part in range(2):
                     for k in range(1, 4):
                         arrived(final_copies[part][k - 1 : k])
-                        other = 2 * lax.rem(z - k + 4, 4) + c
+                        other = 2 * mirrored(lax.rem(z - k + 4, 4)) + c
                         rows = pl.ds(pl.multiple_of(OWN * other, OWN), OWN)
                         spot = out_obj.at[part, rows]
                         sibling_copies.append(send(spot, spot, t, sibling))

time: 142 us -> 138 us (0.972)
  Pallas kernels: 132 us -> 129 us
    pallas_call x1, Pallas kernels: 132 us -> 129 us  [shards(): pl.pallas_call(body, name='refine', out_shape=(jax.ShapeDtypeStruct(objec...]
where the time goes in v5:
time: 138 us
  Pallas kernels  129 us (93%)
  local copies, waits for them, and re-layouts  8.19 us (6%)
    pallas_call x1, Pallas kernels, shards(): pl.pallas_call(body, name='refine', out_shape=(jax.ShapeDtypeStruct(objec...  129 us
    unnamed x14, local copies, waits for them, and re-layouts  8.19 us

profile of v5, /device:TPU:1, one launch (start us, length us, event | category | flops | bytes accessed | tf_op | source)
XLA Modules:
  0.0 137.8 jit_solution(11681131359092346019)
XLA Ops:
  0.6 0.0 copy-start
  0.6 1.2 copy-done
  1.9 0.0 copy-start.1
  1.9 1.2 copy-done.1
  3.1 0.0 copy-start.2
  3.1 1.1 copy-done.2
  4.2 0.0 copy-start.3
  4.2 1.1 copy-done.3
  5.3 0.0 copy-start.4
  5.4 1.0 copy-done.4
  6.4 0.0 copy-start.5
  6.4 0.7 copy-done.5
  7.1 129.0 %refine.1 = (f32[2,256,512]{2,1,0:T(8,128)S(1)}, f32[1,2,256,256]{3,2,1,0:T(8,128)S(1)}) custom-call(s32[2,2,2]{2,1,0:T(2,128)S(1)} %copy-done.5, f32[2,256,512]{2,1,0:T(8,128)S(1)} %copy-done, f32[1,2,256,256]{3,2,1,0:T(8,128)S(1)} %copy-done.4, f32[2,2,256,256]{3,2,1,0:T(8,128)S(1)} %copy-done.1, bf16[768,512]{1,0:T(8,128)(2,1)S(1)} %copy-done.3, ...), custom_call_target="tpu_custom_call" | custom-call | tf_op jit(solution)/shard_map/refine/pallas_call | solution.py:710
  136.1 1.0 copy.10
  137.1 0.8 copy.11
Async XLA Ops:
  0.6 1.2 copy-start
  1.9 1.2 copy-start.1
  3.1 1.1 copy-start.2
  4.2 1.1 copy-start.3
  5.3 1.0 copy-start.4
  6.4 0.7 copy-start.5

commit v6 on v5

--- a/solution.py
+++ b/solution.py
@@ -105,6 +105,7 @@
         where_own=pltpu.VMEM((8, N), jnp.int32),
         where_minus=pltpu.VMEM((8, N), jnp.int32),
         where_plus=pltpu.VMEM((8, N), jnp.int32),
+        strip=pltpu.VMEM((2, N, WIDTH), F32),
         rolled=pltpu.VMEM((2, 2, N, N), F32),
         far=pltpu.VMEM((2, 2, N, N), F32),
         stage=pltpu.VMEM((2, 3 * N, 2 * N), BF16),
@@ -122,7 +123,7 @@
 COPIES = 248
 
 
-def kernel(tree, pos, obj, probe, measured, rtable, ltable, out_obj, out_probe, *scratch):
+def kernel(tree, pos, object_field, probe, measured, rtable, ltable, out_obj, out_probe, *scratch):
     ssem, rsem, lsem = scratch[-3:]
     com, *mem = [Box(entries) for entries in jax.tree.unflatten(tree, scratch[:-3])]
     t = lax.axis_index("tile")
@@ -146,6 +147,13 @@
     own_row = pl.multiple_of(OWN * block, OWN)
     i_row = pl.multiple_of(64 * z, 64)
     sent = []
+    obj = com.strip
+    first_loads = [
+        pltpu.make_async_copy(object_field, obj, lsem.at[4]),
+        pltpu.make_async_copy(probe.at[0], mem[0].probes.at[0, pl.ds(0, 2)], lsem.at[5]),
+    ]
+    for load in first_loads:
+        load.start()
 
     def send(src, dst, tile, mode):
         index = len(sent)
@@ -199,8 +207,8 @@
             com.where_own[4 * b + 2 * j + 1 : 4 * b + 2 * j + 2, :] = jnp.full(
                 (1, N), column, jnp.int32
             )
-    for part in range(2):
-        mem[0].probes[0, part] = probe[0, part]
+    for load in first_loads:
+        load.wait()
     pl.semaphore_wait(barrier, len(partners))
 
     def place(ref, b, j):
@@ -369,13 +377,12 @@
         moved = dot(jnp.concatenate([high, low], axis=1), jnp.concatenate([pick, pick], axis=0))
         return moved[:N], moved[N:]
 
-    def roll_probes(b):
+    def roll_probe(b, mode):
         row, column = place(com.where_own, b, 0)
         probes = mem[b].probes
-        for mode in range(2):
-            rolled[mode, 0], rolled[mode, 1] = shifted(
-                probes[mode, 0], probes[mode, 1], -row, -column
-            )
+        rolled[mode, 0], rolled[mode, 1] = shifted(
+            probes[mode, 0], probes[mode, 1], -row, -column
+        )
 
     def unroll_step(b, mode):
         row, column = place(com.where_own, b, 0)
@@ -561,10 +568,10 @@
         halo_copy = send(obj.at[:, pl.ds(own_row, OWN)], mem[0].halo, t_minus, facing(t_minus))
         arrived(edge_copies)
         patch_copies = send_edges()
-        arrived([probe_copy])
-        roll_probes(0)
+        roll_probe(0, 0)
+        mine = mem[0].probes.at[0]
         power_copies = send_power(
-            0, [(probe[0, 0, held[part]], probe[0, 1, held[part]]) for part in range(2)]
+            0, [(mine[0, held[part]], mine[1, held[part]]) for part in range(2)]
         )
         arrived(where_copies)
         for load in loads:
@@ -575,12 +582,13 @@
                 field, field_rows = obj, pl.ds(own_row, OWN)
             else:
                 field, field_rows = mem[b - 1].objnew, slice(0, OWN)
+            if b:
+                roll_probe(b, 0)
+            arrived([probe_copy])
+            roll_probe(b, 1)
             arrived(patch_copies)
             if b == 0:
                 join_edges()
-            if b:
-                arrived([probe_copy])
-                roll_probes(b)
             copies = forward(b)
             sum_power(b, power_copies)
             power_gather = Gather(lambda rows: mem[b].probes.at[0, 2, rows])
@@ -706,7 +714,7 @@
         kernel(tree, *refs)
 
     vmem = pl.BlockSpec(memory_space=pltpu.VMEM)
-    anywhere = pl.BlockSpec(memory_space=pl.ANY)
+    main = pl.BlockSpec(memory_space=pltpu.HBM)
     return pl.pallas_call(
         body,
         name="refine",
@@ -714,10 +722,10 @@
             jax.ShapeDtypeStruct(object_field.shape, F32),
             jax.ShapeDtypeStruct(probe.shape, F32),
         ),
-        in_specs=[pl.BlockSpec(memory_space=pltpu.SMEM)] + [vmem] * 2 + [anywhere] * 3,
+        in_specs=[pl.BlockSpec(memory_space=pltpu.SMEM)] + [main] * 5,
         out_specs=(vmem, vmem),
         scratch_shapes=leaves
-        + [pltpu.SemaphoreType.DMA((count,)) for count in (COPIES, COPIES, 4)],
+        + [pltpu.SemaphoreType.DMA((count,)) for count in (COPIES, COPIES, 6)],
         compiler_params=pltpu.CompilerParams(
             collective_id=0, has_side_effects=True, vmem_limit_bytes=30 * 1024 * 1024
         ),

time: 138 us -> 137 us (level)
  no operation moved by 1% of the time
where the time goes in v6:
time: 137 us
  Pallas kernels  128 us (93%)
  local copies, waits for them, and re-layouts  8.19 us (6%)
    pallas_call x1, Pallas kernels, shards(): pl.pallas_call(body, name='refine', out_shape=(jax.ShapeDtypeStruct(objec...  128 us
    unnamed x14, local copies, waits for them, and re-layouts  8.19 us

profile of v6, /device:TPU:1, one launch (start us, length us, event | category | flops | bytes accessed | tf_op | source)
XLA Modules:
  0.0 137.1 jit_solution(2969704153406468830)
XLA Ops:
  0.6 0.0 copy-start
  0.6 1.2 copy-done
  1.9 0.0 copy-start.1
  1.9 1.2 copy-done.1
  3.1 0.0 copy-start.2
  3.1 1.1 copy-done.2
  4.2 0.0 copy-start.3
  4.2 1.1 copy-done.3
  5.3 0.0 copy-start.4
  5.4 1.0 copy-done.4
  6.4 0.0 copy-start.5
  6.4 0.7 copy-done.5
  7.1 128.2 %refine.1 = (f32[2,256,512]{2,1,0:T(8,128)S(1)}, f32[1,2,256,256]{3,2,1,0:T(8,128)S(1)}) custom-call(s32[2,2,2]{2,1,0:T(2,128)S(1)} %copy-done.5, f32[2,256,512]{2,1,0:T(8,128)S(1)} %copy-done, f32[1,2,256,256]{3,2,1,0:T(8,128)S(1)} %copy-done.4, f32[2,2,256,256]{3,2,1,0:T(8,128)S(1)} %copy-done.1, bf16[768,512]{1,0:T(8,128)(2,1)S(1)} %copy-done.3, ...), custom_call_target="tpu_custom_call" | custom-call | tf_op jit(solution)/shard_map/refine/pallas_call | solution.py:718
  135.3 1.0 copy.10
  136.3 0.8 copy.11
Async XLA Ops:
  0.6 1.2 copy-start
  1.9 1.2 copy-start.1
  3.1 1.1 copy-start.2
  4.2 1.1 copy-start.3
  5.3 1.0 copy-start.4
  6.4 0.7 copy-start.5

commit v7 on v6

--- a/solution.py
+++ b/solution.py
@@ -565,14 +565,11 @@
             send(com.where_own, com.where_minus, t_plus, facing(t_plus)),
             send(com.where_own, com.where_plus, t_minus, facing(t_minus)),
         ]
-        halo_copy = send(obj.at[:, pl.ds(own_row, OWN)], mem[0].halo, t_minus, facing(t_minus))
         arrived(edge_copies)
         patch_copies = send_edges()
         roll_probe(0, 0)
         mine = mem[0].probes.at[0]
-        power_copies = send_power(
-            0, [(mine[0, held[part]], mine[1, held[part]]) for part in range(2)]
-        )
+        power_values = [(mine[0, held[part]], mine[1, held[part]]) for part in range(2)]
         arrived(where_copies)
         for load in loads:
             load.wait()
@@ -587,6 +584,10 @@
             arrived([probe_copy])
             roll_probe(b, 1)
             arrived(patch_copies)
+            power_copies = send_power(b, power_values)
+            if b == 0:
+                rows = pl.ds(own_row, OWN)
+                halo_copy = send(obj.at[:, rows], mem[0].halo, t_minus, facing(t_minus))
             if b == 0:
                 join_edges()
             copies = forward(b)
@@ -694,7 +695,7 @@
                 gather.finish()
                 arrived(sibling_copies)
             else:
-                power_copies = send_power(b + 1, values)
+                power_values = values
                 gather.finish()
                 probe_copy = send(
                     following.at[0, pl.ds(0, 2)], following.at[1, pl.ds(0, 2)], t, sibling

time: 137 us -> 135 us (0.985)
  Pallas kernels: 128 us -> 125 us
    pallas_call x1, Pallas kernels: 128 us -> 125 us  [shards(): pl.pallas_call(body, name='refine', out_shape=(jax.ShapeDtypeStruct(objec...]
where the time goes in v7:
time: 135 us; the launch traced here: 134 us
  Pallas kernels  125 us (93%)
  local copies, waits for them, and re-layouts  8.19 us (6%)
    pallas_call x1, Pallas kernels, shards(): pl.pallas_call(body, name='refine', out_shape=(jax.ShapeDtypeStruct(objec...  125 us
    unnamed x14, local copies, waits for them, and re-layouts  8.19 us

profile of v7, /device:TPU:1, one launch (start us, length us, event | category | flops | bytes accessed | tf_op | source)
XLA Modules:
  0.0 133.8 jit_solution(12004075251587071383)
XLA Ops:
  0.6 0.0 copy-start
  0.6 1.2 copy-done
  1.9 0.0 copy-start.1
  1.9 1.2 copy-done.1
  3.1 0.0 copy-start.2
  3.1 1.1 copy-done.2
  4.2 0.0 copy-start.3
  4.2 1.1 copy-done.3
  5.3 0.0 copy-start.4
  5.4 1.0 copy-done.4
  6.4 0.0 copy-start.5
  6.4 0.7 copy-done.5
  7.1 124.9 %refine.1 = (f32[2,256,512]{2,1,0:T(8,128)S(1)}, f32[1,2,256,256]{3,2,1,0:T(8,128)S(1)}) custom-call(s32[2,2,2]{2,1,0:T(2,128)S(1)} %copy-done.5, f32[2,256,512]{2,1,0:T(8,128)S(1)} %copy-done, f32[1,2,256,256]{3,2,1,0:T(8,128)S(1)} %copy-done.4, f32[2,2,256,256]{3,2,1,0:T(8,128)S(1)} %copy-done.1, bf16[768,512]{1,0:T(8,128)(2,1)S(1)} %copy-done.3, ...), custom_call_target="tpu_custom_call" | custom-call | tf_op jit(solution)/shard_map/refine/pallas_call | solution.py:719
  132.0 1.0 copy.10
  133.0 0.8 copy.11
Async XLA Ops:
  0.6 1.2 copy-start
  1.9 1.2 copy-start.1
  3.1 1.1 copy-start.2
  4.2 1.1 copy-start.3
  5.3 1.0 copy-start.4
  6.4 0.7 copy-start.5
